TPU v7x, 512 devices: a whole 4x4x16 slice. The times are simulated.
512 devices in a mesh: blk: 16 (over y_hi, x, core), wide: 32 (over y_lo, z).
Axes of the slice: x: 4, y: 4 (y_hi: 2, y_lo: 2; y = y_hi * 2 + y_lo), z: 16, core: 2. Of those that a mesh axis runs over, the one named last changes fastest.
Arguments:
- patch_keys: float32 [512, 196, 512], P(('blk', 'wide')), may hold values from -16 to 16
- patch_values: float32 [512, 196, 512], P(('blk', 'wide')), may hold values from -6 to 6
- caption_queries: float32 [512, 512], P(('blk', 'wide')), may hold values from -48 to 48
- positive: int32 [512, 512], P(('blk', 'wide')), may hold values 0 or 1
Outputs:
- grad_keys: float32 [512, 196, 512], P(('blk', 'wide'))
- grad_values: float32 [512, 196, 512], P(('blk', 'wide'))
- grad_queries: float32 [512, 512], P(('blk', 'wide'))
All inputs are finite; a program needn't handle non-finite values. No bound on the sum of `positive` on one device may be relied on, other than what follows from the above.
Results may differ from a plain program's by a relative error of at most 0.0005.
Values sent between devices are 32-bit elements; how exact they have to be, the bound alone decides.
No kernel may reach another device: no remote copies, remote signals or barrier semaphores. Data moves between devices by JAX's collectives and lax.ppermute only.
A program may use at most 64 MiB of HBM per device.

v0:
```python
import jax
import jax.numpy as jnp
from jax import lax
from jax.sharding import PartitionSpec as P

HEADS = 8


epsilon = 1e-06
similarity_multiplier = 10.0
similarity_shift_term = -2.0


def passed_along(value, axis, steps):
    count = lax.axis_size(axis)
    pairs = [(source, (source + steps) % count) for source in range(count)]
    return lax.ppermute(value, axis, pairs)


def pair_loss(keys, values, queries, labels):
    images, patches, width = keys.shape
    row_count = queries.shape[0]
    head_dim = width // HEADS
    query_heads = queries.reshape(row_count, HEADS, head_dim)
    key_heads = keys.reshape(images, patches, HEADS, head_dim)
    value_heads = values.reshape(images, patches, HEADS, head_dim)
    scores = jnp.einsum(
        "chd,iphd->ichp", query_heads, key_heads, precision=lax.Precision.HIGHEST
    ) * head_dim ** (-0.5)
    row_max = lax.stop_gradient(jnp.max(scores, axis=3, keepdims=True))
    exponent = jnp.exp(scores - row_max)
    weights = exponent / jnp.sum(exponent, axis=3, keepdims=True)
    pooled = jnp.einsum(
        "ichp,iphd->ichd", weights, value_heads, precision=lax.Precision.HIGHEST
    ).reshape(images, row_count, width)
    matching_similarity = jnp.mean(pooled * queries[None], axis=2)
    summary_reciprocal_length = lax.rsqrt(jnp.mean(pooled * pooled, axis=2) + epsilon)
    probe_reciprocal_length = lax.rsqrt(jnp.mean(queries * queries, axis=1) + epsilon)
    matching_scaled_scores = (
        similarity_multiplier
        * matching_similarity
        * summary_reciprocal_length
        * probe_reciprocal_length[None]
        + similarity_shift_term
    )
    label_signs = 2.0 * labels.astype(jnp.float32) - 1.0
    return jnp.sum(jnp.logaddexp(0.0, -label_signs * matching_scaled_scores))


def pair_grads(keys, values, queries, labels):

    def loss_of(keys_in, values_in, input_queries):
        return pair_loss(keys_in, values_in, input_queries, labels)

    total, pull_back = jax.vjp(loss_of, keys, values, queries)
    return pull_back(jnp.ones_like(total))


def per_device(patch_keys, patch_values, caption_queries, positive):
    caption_group = lax.all_gather(caption_queries, "wide", axis=0, tiled=True)
    group_rows = caption_group.shape[0]
    cycle_size = lax.axis_size("blk")
    cycle_home = lax.axis_index("blk")
    key_zero = jnp.zeros_like(patch_keys)
    value_zero = jnp.zeros_like(patch_values)

    def cycle_turn(turn, carried):
        key_grad, value_grad, evaluate_objective, forward_acc, backward, backward_acc = carried
        source = (cycle_home - turn) % cycle_size
        labels_fwd = lax.dynamic_slice_in_dim(positive, source * group_rows, group_rows, 1)
        visiting = evaluate_objective
        key_part, value_part, query_part = pair_grads(
            patch_keys, patch_values, visiting, labels_fwd
        )
        forward_acc = forward_acc + query_part
        backward_acc = backward_acc + query_part[group_rows:]
        evaluate_objective, forward_acc = passed_along((evaluate_objective, forward_acc), "blk", 1)
        return (
            key_grad + key_part,
            value_grad + value_part,
            evaluate_objective,
            forward_acc,
            backward,
            backward_acc,
        )

    backward_start = caption_group[group_rows:]
    initial = (
        key_zero,
        value_zero,
        caption_group,
        jnp.zeros_like(caption_group),
        backward_start,
        jnp.zeros_like(backward_start),
    )
    grad_keys, grad_values, forward_end, forward_acc, backward_end, backward_acc = lax.fori_loop(
        0, cycle_size, cycle_turn, initial
    )
    group_grad = jnp.concatenate([forward_acc, backward_acc], 0)
    grad_queries = lax.psum_scatter(group_grad, "wide", scatter_dimension=0, tiled=True)
    return (grad_keys, grad_values, grad_queries)


def solution(mesh):
    in_specs = (
        P(("blk", "wide"), None, None),
        P(("blk", "wide"), None, None),
        P(("blk", "wide"), None),
        P(("blk", "wide"), None),
    )
    out_specs = (
        P(("blk", "wide"), None, None),
        P(("blk", "wide"), None, None),
        P(("blk", "wide"), None),
    )
    return jax.shard_map(
        per_device, mesh=mesh, in_specs=in_specs, out_specs=out_specs, check_vma=False
    )
```

profile of v0, /device:TPU:2, one launch (start us, length us, event | category | flops | bytes accessed | tf_op | source)
XLA Modules:
  0.0 610.4 jit_solution(129645985034968549)
XLA Ops:
  9.2 69.2 %all-gather = f32[32,1,512]{2,1,0:T(1,128)S(1)} all-gather(f32[1,1,512]{2,1,0:T(1,128)S(1)} %bitcast.248), channel_id=1, replica_groups=mesh['blk'=16,'wide'=32] {'wide'}, dimensions={0}, use_global_device_ids=true | all-gather | bytes 67584 | tf_op jit(solution)/shard_map/all_gather | solution.py:60
  79.6 283.0 %while.23 = (s32[]{:T(128)}, f32[1,196,512]{1,2,0:T(8,128)S(1)}, f32[1,196,512]{1,2,0:T(8,128)S(1)}, f32[32,512]{1,0:T(8,128)}, f32[32,512]{1,0:T(8,128)}, /*ind...) while((s32[]{:T(128)}, f32[1,196,512]{1,2,0:T(8,128)S(1)}, ...), condition=%wide.region_7.8_spmd.clone, body=%wide.region_0.7_spmd.clone.sunk | while | flops 232979744 | bytes 9337618 | solution.py:96
  88.2 3.5 collective-permute-start.1
  96.3 1.9 collective-permute-start
  104.0 3.2 collective-permute-start.1
  111.8 1.9 collective-permute-start
  119.5 4.8 collective-permute-start.1
  128.9 1.9 collective-permute-start
  136.6 5.7 collective-permute-start.1
  147.0 1.9 collective-permute-start
  154.7 5.7 collective-permute-start.1
  165.0 1.9 collective-permute-start
  172.7 5.7 collective-permute-start.1
  183.1 1.9 collective-permute-start
  190.8 5.7 collective-permute-start.1
  201.1 1.9 collective-permute-start
  208.8 5.7 collective-permute-start.1
  219.2 1.9 collective-permute-start
  226.8 5.7 collective-permute-start.1
  237.2 1.9 collective-permute-start
  244.9 5.7 collective-permute-start.1
  255.2 1.9 collective-permute-start
  262.9 5.7 collective-permute-start.1
  281.0 5.7 collective-permute-start.1
  291.3 1.9 collective-permute-start
  299.0 5.7 collective-permute-start.1
  309.4 1.9 collective-permute-start
  317.1 5.7 collective-permute-start.1
  335.1 5.7 collective-permute-start.1
  345.5 1.9 collective-permute-start
  353.2 5.7 collective-permute-start.1
  366.0 235.7 %all-reduce.3.cloned.1.call-done = f32[32,512]{1,0:T(8,128)} async-done(((f32[32,512]{1,0:T(8,128)}), f32[32,512]{1,0:T(8,128)}) %all-reduce.3.cloned.1.call-update) | async-done | bytes 65552
  (403 shorter events, 177.8 us)
Async XLA Ops:
  7.2 594.5 %all-reduce.3.cloned.1.call-start = ((), (), s32[]{:S(2)}) async-start(), calls=%async_computation | async-start | bytes 131072
  80.5 14.9 %collective-permute-start = (f32[32,512]{1,0:T(8,128)S(1)}, f32[32,512]{1,0:T(8,128)}, u32[]{:S(2)}, u32[]{:S(2)}) collective-permute-start(f32[32,512]{1,0:T(8,128)S(1)} %copy.71), channel_id=1, source_target_pairs={{0,32},{32,64},{64,96},{96,128},{128,160},{160,192},{192,224},{224... | collective-permute-start | bytes 196616 | tf_op jit(solution)/shard_map/while/body/eval_jaxpr/ppermute | solution.py:17
  88.2 7.2 %collective-permute-start.1 = (f32[32,512]{1,0:T(8,128)}, f32[32,512]{1,0:T(8,128)}, u32[]{:S(2)}, u32[]{:S(2)}) collective-permute-start(f32[32,512]{1,0:T(8,128)} %fusion.71), channel_id=1, source_target_pairs={{0,32},{32,64},{64,96},{96,128},{128,160},{160,192},{192,224},{224... | collective-permute-start | bytes 196616 | tf_op jit(solution)/shard_map/while/body/eval_jaxpr/ppermute | solution.py:17
  96.3 14.7 %collective-permute-start = (f32[32,512]{1,0:T(8,128)S(1)}, f32[32,512]{1,0:T(8,128)}, u32[]{:S(2)}, u32[]{:S(2)}) collective-permute-start(f32[32,512]{1,0:T(8,128)S(1)} %copy.71), channel_id=1, source_target_pairs={{0,32},{32,64},{64,96},{96,128},{128,160},{160,192},{192,224},{224... | collective-permute-start | bytes 196616 | tf_op jit(solution)/shard_map/while/body/eval_jaxpr/ppermute | solution.py:17
  111.8 16.3 %collective-permute-start = (f32[32,512]{1,0:T(8,128)S(1)}, f32[32,512]{1,0:T(8,128)}, u32[]{:S(2)}, u32[]{:S(2)}) collective-permute-start(f32[32,512]{1,0:T(8,128)S(1)} %copy.71), channel_id=1, source_target_pairs={{0,32},{32,64},{64,96},{96,128},{128,160},{160,192},{192,224},{224... | collective-permute-start | bytes 196616 | tf_op jit(solution)/shard_map/while/body/eval_jaxpr/ppermute | solution.py:17
  119.5 8.6 %collective-permute-start.1 = (f32[32,512]{1,0:T(8,128)}, f32[32,512]{1,0:T(8,128)}, u32[]{:S(2)}, u32[]{:S(2)}) collective-permute-start(f32[32,512]{1,0:T(8,128)} %fusion.71), channel_id=1, source_target_pairs={{0,32},{32,64},{64,96},{96,128},{128,160},{160,192},{192,224},{224... | collective-permute-start | bytes 196616 | tf_op jit(solution)/shard_map/while/body/eval_jaxpr/ppermute | solution.py:17
  128.9 17.2 %collective-permute-start = (f32[32,512]{1,0:T(8,128)S(1)}, f32[32,512]{1,0:T(8,128)}, u32[]{:S(2)}, u32[]{:S(2)}) collective-permute-start(f32[32,512]{1,0:T(8,128)S(1)} %copy.71), channel_id=1, source_target_pairs={{0,32},{32,64},{64,96},{96,128},{128,160},{160,192},{192,224},{224... | collective-permute-start | bytes 196616 | tf_op jit(solution)/shard_map/while/body/eval_jaxpr/ppermute | solution.py:17
  136.6 9.5 %collective-permute-start.1 = (f32[32,512]{1,0:T(8,128)}, f32[32,512]{1,0:T(8,128)}, u32[]{:S(2)}, u32[]{:S(2)}) collective-permute-start(f32[32,512]{1,0:T(8,128)} %fusion.71), channel_id=1, source_target_pairs={{0,32},{32,64},{64,96},{96,128},{128,160},{160,192},{192,224},{224... | collective-permute-start | bytes 196616 | tf_op jit(solution)/shard_map/while/body/eval_jaxpr/ppermute | solution.py:17
  147.0 17.2 %collective-permute-start = (f32[32,512]{1,0:T(8,128)S(1)}, f32[32,512]{1,0:T(8,128)}, u32[]{:S(2)}, u32[]{:S(2)}) collective-permute-start(f32[32,512]{1,0:T(8,128)S(1)} %copy.71), channel_id=1, source_target_pairs={{0,32},{32,64},{64,96},{96,128},{128,160},{160,192},{192,224},{224... | collective-permute-start | bytes 196616 | tf_op jit(solution)/shard_map/while/body/eval_jaxpr/ppermute | solution.py:17
  154.7 9.5 %collective-permute-start.1 = (f32[32,512]{1,0:T(8,128)}, f32[32,512]{1,0:T(8,128)}, u32[]{:S(2)}, u32[]{:S(2)}) collective-permute-start(f32[32,512]{1,0:T(8,128)} %fusion.71), channel_id=1, source_target_pairs={{0,32},{32,64},{64,96},{96,128},{128,160},{160,192},{192,224},{224... | collective-permute-start | bytes 196616 | tf_op jit(solution)/shard_map/while/body/eval_jaxpr/ppermute | solution.py:17
  165.0 17.2 %collective-permute-start = (f32[32,512]{1,0:T(8,128)S(1)}, f32[32,512]{1,0:T(8,128)}, u32[]{:S(2)}, u32[]{:S(2)}) collective-permute-start(f32[32,512]{1,0:T(8,128)S(1)} %copy.71), channel_id=1, source_target_pairs={{0,32},{32,64},{64,96},{96,128},{128,160},{160,192},{192,224},{224... | collective-permute-start | bytes 196616 | tf_op jit(solution)/shard_map/while/body/eval_jaxpr/ppermute | solution.py:17
  172.7 9.5 %collective-permute-start.1 = (f32[32,512]{1,0:T(8,128)}, f32[32,512]{1,0:T(8,128)}, u32[]{:S(2)}, u32[]{:S(2)}) collective-permute-start(f32[32,512]{1,0:T(8,128)} %fusion.71), channel_id=1, source_target_pairs={{0,32},{32,64},{64,96},{96,128},{128,160},{160,192},{192,224},{224... | collective-permute-start | bytes 196616 | tf_op jit(solution)/shard_map/while/body/eval_jaxpr/ppermute | solution.py:17
  183.1 17.2 %collective-permute-start = (f32[32,512]{1,0:T(8,128)S(1)}, f32[32,512]{1,0:T(8,128)}, u32[]{:S(2)}, u32[]{:S(2)}) collective-permute-start(f32[32,512]{1,0:T(8,128)S(1)} %copy.71), channel_id=1, source_target_pairs={{0,32},{32,64},{64,96},{96,128},{128,160},{160,192},{192,224},{224... | collective-permute-start | bytes 196616 | tf_op jit(solution)/shard_map/while/body/eval_jaxpr/ppermute | solution.py:17
  190.8 9.5 %collective-permute-start.1 = (f32[32,512]{1,0:T(8,128)}, f32[32,512]{1,0:T(8,128)}, u32[]{:S(2)}, u32[]{:S(2)}) collective-permute-start(f32[32,512]{1,0:T(8,128)} %fusion.71), channel_id=1, source_target_pairs={{0,32},{32,64},{64,96},{96,128},{128,160},{160,192},{192,224},{224... | collective-permute-start | bytes 196616 | tf_op jit(solution)/shard_map/while/body/eval_jaxpr/ppermute | solution.py:17
  201.1 17.2 %collective-permute-start = (f32[32,512]{1,0:T(8,128)S(1)}, f32[32,512]{1,0:T(8,128)}, u32[]{:S(2)}, u32[]{:S(2)}) collective-permute-start(f32[32,512]{1,0:T(8,128)S(1)} %copy.71), channel_id=1, source_target_pairs={{0,32},{32,64},{64,96},{96,128},{128,160},{160,192},{192,224},{224... | collective-permute-start | bytes 196616 | tf_op jit(solution)/shard_map/while/body/eval_jaxpr/ppermute | solution.py:17
  208.8 9.5 %collective-permute-start.1 = (f32[32,512]{1,0:T(8,128)}, f32[32,512]{1,0:T(8,128)}, u32[]{:S(2)}, u32[]{:S(2)}) collective-permute-start(f32[32,512]{1,0:T(8,128)} %fusion.71), channel_id=1, source_target_pairs={{0,32},{32,64},{64,96},{96,128},{128,160},{160,192},{192,224},{224... | collective-permute-start | bytes 196616 | tf_op jit(solution)/shard_map/while/body/eval_jaxpr/ppermute | solution.py:17
  219.2 17.2 %collective-permute-start = (f32[32,512]{1,0:T(8,128)S(1)}, f32[32,512]{1,0:T(8,128)}, u32[]{:S(2)}, u32[]{:S(2)}) collective-permute-start(f32[32,512]{1,0:T(8,128)S(1)} %copy.71), channel_id=1, source_target_pairs={{0,32},{32,64},{64,96},{96,128},{128,160},{160,192},{192,224},{224... | collective-permute-start | bytes 196616 | tf_op jit(solution)/shard_map/while/body/eval_jaxpr/ppermute | solution.py:17
  226.8 9.5 %collective-permute-start.1 = (f32[32,512]{1,0:T(8,128)}, f32[32,512]{1,0:T(8,128)}, u32[]{:S(2)}, u32[]{:S(2)}) collective-permute-start(f32[32,512]{1,0:T(8,128)} %fusion.71), channel_id=1, source_target_pairs={{0,32},{32,64},{64,96},{96,128},{128,160},{160,192},{192,224},{224... | collective-permute-start | bytes 196616 | tf_op jit(solution)/shard_map/while/body/eval_jaxpr/ppermute | solution.py:17
  237.2 17.2 %collective-permute-start = (f32[32,512]{1,0:T(8,128)S(1)}, f32[32,512]{1,0:T(8,128)}, u32[]{:S(2)}, u32[]{:S(2)}) collective-permute-start(f32[32,512]{1,0:T(8,128)S(1)} %copy.71), channel_id=1, source_target_pairs={{0,32},{32,64},{64,96},{96,128},{128,160},{160,192},{192,224},{224... | collective-permute-start | bytes 196616 | tf_op jit(solution)/shard_map/while/body/eval_jaxpr/ppermute | solution.py:17
  244.9 9.5 %collective-permute-start.1 = (f32[32,512]{1,0:T(8,128)}, f32[32,512]{1,0:T(8,128)}, u32[]{:S(2)}, u32[]{:S(2)}) collective-permute-start(f32[32,512]{1,0:T(8,128)} %fusion.71), channel_id=1, source_target_pairs={{0,32},{32,64},{64,96},{96,128},{128,160},{160,192},{192,224},{224... | collective-permute-start | bytes 196616 | tf_op jit(solution)/shard_map/while/body/eval_jaxpr/ppermute | solution.py:17
  255.2 17.2 %collective-permute-start = (f32[32,512]{1,0:T(8,128)S(1)}, f32[32,512]{1,0:T(8,128)}, u32[]{:S(2)}, u32[]{:S(2)}) collective-permute-start(f32[32,512]{1,0:T(8,128)S(1)} %copy.71), channel_id=1, source_target_pairs={{0,32},{32,64},{64,96},{96,128},{128,160},{160,192},{192,224},{224... | collective-permute-start | bytes 196616 | tf_op jit(solution)/shard_map/while/body/eval_jaxpr/ppermute | solution.py:17
  262.9 9.5 %collective-permute-start.1 = (f32[32,512]{1,0:T(8,128)}, f32[32,512]{1,0:T(8,128)}, u32[]{:S(2)}, u32[]{:S(2)}) collective-permute-start(f32[32,512]{1,0:T(8,128)} %fusion.71), channel_id=1, source_target_pairs={{0,32},{32,64},{64,96},{96,128},{128,160},{160,192},{192,224},{224... | collective-permute-start | bytes 196616 | tf_op jit(solution)/shard_map/while/body/eval_jaxpr/ppermute | solution.py:17
  273.3 17.2 %collective-permute-start = (f32[32,512]{1,0:T(8,128)S(1)}, f32[32,512]{1,0:T(8,128)}, u32[]{:S(2)}, u32[]{:S(2)}) collective-permute-start(f32[32,512]{1,0:T(8,128)S(1)} %copy.71), channel_id=1, source_target_pairs={{0,32},{32,64},{64,96},{96,128},{128,160},{160,192},{192,224},{224... | collective-permute-start | bytes 196616 | tf_op jit(solution)/shard_map/while/body/eval_jaxpr/ppermute | solution.py:17
  281.0 9.5 %collective-permute-start.1 = (f32[32,512]{1,0:T(8,128)}, f32[32,512]{1,0:T(8,128)}, u32[]{:S(2)}, u32[]{:S(2)}) collective-permute-start(f32[32,512]{1,0:T(8,128)} %fusion.71), channel_id=1, source_target_pairs={{0,32},{32,64},{64,96},{96,128},{128,160},{160,192},{192,224},{224... | collective-permute-start | bytes 196616 | tf_op jit(solution)/shard_map/while/body/eval_jaxpr/ppermute | solution.py:17
  291.3 17.2 %collective-permute-start = (f32[32,512]{1,0:T(8,128)S(1)}, f32[32,512]{1,0:T(8,128)}, u32[]{:S(2)}, u32[]{:S(2)}) collective-permute-start(f32[32,512]{1,0:T(8,128)S(1)} %copy.71), channel_id=1, source_target_pairs={{0,32},{32,64},{64,96},{96,128},{128,160},{160,192},{192,224},{224... | collective-permute-start | bytes 196616 | tf_op jit(solution)/shard_map/while/body/eval_jaxpr/ppermute | solution.py:17
  299.0 9.5 %collective-permute-start.1 = (f32[32,512]{1,0:T(8,128)}, f32[32,512]{1,0:T(8,128)}, u32[]{:S(2)}, u32[]{:S(2)}) collective-permute-start(f32[32,512]{1,0:T(8,128)} %fusion.71), channel_id=1, source_target_pairs={{0,32},{32,64},{64,96},{96,128},{128,160},{160,192},{192,224},{224... | collective-permute-start | bytes 196616 | tf_op jit(solution)/shard_map/while/body/eval_jaxpr/ppermute | solution.py:17
  309.4 17.2 %collective-permute-start = (f32[32,512]{1,0:T(8,128)S(1)}, f32[32,512]{1,0:T(8,128)}, u32[]{:S(2)}, u32[]{:S(2)}) collective-permute-start(f32[32,512]{1,0:T(8,128)S(1)} %copy.71), channel_id=1, source_target_pairs={{0,32},{32,64},{64,96},{96,128},{128,160},{160,192},{192,224},{224... | collective-permute-start | bytes 196616 | tf_op jit(solution)/shard_map/while/body/eval_jaxpr/ppermute | solution.py:17
  317.1 9.5 %collective-permute-start.1 = (f32[32,512]{1,0:T(8,128)}, f32[32,512]{1,0:T(8,128)}, u32[]{:S(2)}, u32[]{:S(2)}) collective-permute-start(f32[32,512]{1,0:T(8,128)} %fusion.71), channel_id=1, source_target_pairs={{0,32},{32,64},{64,96},{96,128},{128,160},{160,192},{192,224},{224... | collective-permute-start | bytes 196616 | tf_op jit(solution)/shard_map/while/body/eval_jaxpr/ppermute | solution.py:17
  327.4 17.2 %collective-permute-start = (f32[32,512]{1,0:T(8,128)S(1)}, f32[32,512]{1,0:T(8,128)}, u32[]{:S(2)}, u32[]{:S(2)}) collective-permute-start(f32[32,512]{1,0:T(8,128)S(1)} %copy.71), channel_id=1, source_target_pairs={{0,32},{32,64},{64,96},{96,128},{128,160},{160,192},{192,224},{224... | collective-permute-start | bytes 196616 | tf_op jit(solution)/shard_map/while/body/eval_jaxpr/ppermute | solution.py:17
  335.1 9.5 %collective-permute-start.1 = (f32[32,512]{1,0:T(8,128)}, f32[32,512]{1,0:T(8,128)}, u32[]{:S(2)}, u32[]{:S(2)}) collective-permute-start(f32[32,512]{1,0:T(8,128)} %fusion.71), channel_id=1, source_target_pairs={{0,32},{32,64},{64,96},{96,128},{128,160},{160,192},{192,224},{224... | collective-permute-start | bytes 196616 | tf_op jit(solution)/shard_map/while/body/eval_jaxpr/ppermute | solution.py:17
  345.5 17.2 %collective-permute-start = (f32[32,512]{1,0:T(8,128)S(1)}, f32[32,512]{1,0:T(8,128)}, u32[]{:S(2)}, u32[]{:S(2)}) collective-permute-start(f32[32,512]{1,0:T(8,128)S(1)} %copy.71), channel_id=1, source_target_pairs={{0,32},{32,64},{64,96},{96,128},{128,160},{160,192},{192,224},{224... | collective-permute-start | bytes 196616 | tf_op jit(solution)/shard_map/while/body/eval_jaxpr/ppermute | solution.py:17
  353.2 9.5 %collective-permute-start.1 = (f32[32,512]{1,0:T(8,128)}, f32[32,512]{1,0:T(8,128)}, u32[]{:S(2)}, u32[]{:S(2)}) collective-permute-start(f32[32,512]{1,0:T(8,128)} %fusion.71), channel_id=1, source_target_pairs={{0,32},{32,64},{64,96},{96,128},{128,160},{160,192},{192,224},{224... | collective-permute-start | bytes 196616 | tf_op jit(solution)/shard_map/while/body/eval_jaxpr/ppermute | solution.py:17
  (3 other events, 8.9 us)
Sparse Core Ops, SparseCore 0:
  362.8 238.8 all-reduce.2
where the time goes:
time: 614 us; the launch traced here: 610 us
  waiting for transfers between devices  236 us (38%)
  starting transfers between devices  117 us (19%)
  matrix products  76 us (12%)
  blocking collectives  69.2 us (11%)
  other arithmetic  65.8 us (11%)
  local copies, waits for them, and re-layouts  30.2 us (5%)
  between operations  14.1 us (2%)
    unnamed x2, waiting for transfers between devices  236 us
    ppermute x32, starting transfers between devices, passed_along(): return lax.ppermute(value, axis, pairs)  117 us
    all_gather x1, blocking collectives, per_device(): caption_group = lax.all_gather(caption_queries, 'wide', axis=0, tiled=True)  69.2 us
    dot_general x48, matrix products, pair_loss(): jnp.einsum('ichp,iphd->ichd', weights, value_heads, precision=lax.Precisi...  44.3 us
    dot_general x48, matrix products, pair_loss(): jnp.einsum('chd,iphd->ichp', query_heads, key_heads, precision=lax.Precis...  31.7 us
    add x16, other arithmetic, cycle_turn(): forward_acc = forward_acc + query_part  24.8 us
    add x16, other arithmetic, cycle_turn(): value_grad + value_part  22.3 us
    while x16, local copies, waits for them, and re-layouts  13.5 us
  transfers between devices with their start and end apart: 33, of which 1 were waited for; matrix products, arithmetic and copies ran while one was open for 25% of the time, Pallas kernels for 0%

commit v1 on v0

v1 whole, which is shorter than its diff:
```python
import functools
import math

import jax
import jax.numpy as jnp
from jax import lax
from jax.experimental import pallas as pl
from jax.experimental.pallas import tpu as pltpu
from jax.sharding import Mesh
from jax.sharding import PartitionSpec as P

HEADS = 8
HEAD_DIM = 64
ROWS = 208
LOG2E = math.log2(math.e)
LN2 = math.log(2.0)


def split(x):
    high = x.astype(jnp.bfloat16)
    return high, (x - high.astype(jnp.float32)).astype(jnp.bfloat16)


def product(lhs, rhs, transposed=False):
    contract = ((1,), (1 if transposed else 0,))
    return lax.dot_general(lhs, rhs, (contract, ((), ())), preferred_element_type=jnp.float32)


def prepare_kernel(k_ref, v_ref, kc_ref, vc_ref, kt_ref, vt_ref, pad_ref):
    patches = k_ref.shape[0]
    for source, cat_ref, turned_ref in ((k_ref, kc_ref, kt_ref), (v_ref, vc_ref, vt_ref)):
        pad_ref[192:, :] = jnp.zeros((64, 512), jnp.float32)
        pad_ref[:patches, :] = source[...]
        left = lax.broadcasted_iota(jnp.int32, (ROWS, 128), 1) < HEAD_DIM
        for pair in range(HEADS // 2):
            tile = pad_ref[:, pair * 128:(pair + 1) * 128]
            rows = tile[:ROWS]
            high = rows.astype(jnp.bfloat16).astype(jnp.float32)
            for place, part in ((0, high), (1, rows - high)):
                rolled = pltpu.roll(part, HEAD_DIM, 1)
                lanes = slice(place * 128, (place + 1) * 128)
                cat_ref[2 * pair, :, lanes] = jnp.where(left, part, rolled).astype(jnp.bfloat16)
                cat_ref[2 * pair + 1, :, lanes] = jnp.where(left, rolled, part).astype(jnp.bfloat16)
            turned_high, turned_low = split(tile.T)
            for side in range(2):
                own = slice(side * HEAD_DIM, (side + 1) * HEAD_DIM)
                turned_ref[2 * pair + side, :HEAD_DIM, :] = turned_high[own, :ROWS]
                turned_ref[2 * pair + side, HEAD_DIM:, :] = turned_low[own, :ROWS]


def prepare(k, v):
    cat = jax.ShapeDtypeStruct((HEADS, ROWS, 256), jnp.bfloat16)
    turned = jax.ShapeDtypeStruct((HEADS, 128, ROWS), jnp.bfloat16)
    return pl.pallas_call(
        prepare_kernel,
        out_shape=(cat, cat, turned, turned),
        scratch_shapes=[pltpu.VMEM((256, 512), jnp.float32)],
        name="prepare",
    )(k, v)


def chunk_grads(q, label, kc_ref, vc_ref, kt_ref, vt_ref, key_acc, value_acc, e_ref, eh_ref, el_ref, o_ref, first):
    columns = q.shape[0]
    turned = q.T
    query_high, query_low = split(turned * (LOG2E / 8.0))
    inverse = []
    match = jnp.zeros((1, columns), jnp.float32)
    square = jnp.zeros((1, columns), jnp.float32)
    below = lax.broadcasted_iota(jnp.int32, (16, columns), 0) < 4
    for head in range(HEADS):
        own = slice(head * HEAD_DIM, (head + 1) * HEAD_DIM)
        qh, ql = query_high[own], query_low[own]
        scores = product(kc_ref[head], jnp.concatenate([qh, ql, qh, ql], 0))
        scores = jnp.concatenate([scores[:192], jnp.where(below, scores[192:], -1e30)], 0)
        exponent = jnp.exp2(scores - jnp.max(scores, axis=0, keepdims=True))
        inverse.append(1.0 / jnp.sum(exponent, axis=0, keepdims=True))
        high, low = split(exponent)
        e_ref[head] = exponent
        eh_ref[head] = high
        el_ref[head] = low
        wide = product(vt_ref[head], high)
        pooled = (wide[:HEAD_DIM] + wide[HEAD_DIM:] + product(vt_ref[head, :HEAD_DIM], low)) * inverse[head]
        o_ref[own, :] = pooled
        match += jnp.sum(pooled * turned[own], axis=0, keepdims=True)
        square += jnp.sum(pooled * pooled, axis=0, keepdims=True)
    width = HEADS * HEAD_DIM
    match = match / width
    summary = lax.rsqrt(square / width + 1e-6)
    probe = lax.rsqrt(jnp.sum(turned * turned, axis=0, keepdims=True) / width + 1e-6)
    sign = 2.0 * label.astype(jnp.float32) - 1.0
    logit = 10.0 * match * summary * probe - 2.0
    slope = -sign / (1.0 + jnp.exp(sign * logit)) * (10.0 / width)
    alpha = slope * summary * probe
    beta = -alpha * match * summary * summary
    gamma = -alpha * match * probe * probe
    parts = []
    for head in range(HEADS):
        own = slice(head * HEAD_DIM, (head + 1) * HEAD_DIM)
        pooled = o_ref[own, :]
        query = turned[own]
        grad = (alpha * query + beta * pooled) * inverse[head]
        delta = jnp.sum(grad * pooled, axis=0, keepdims=True)
        gh, gl = split(grad)
        inner = product(vc_ref[head], jnp.concatenate([gh, gl, gh, gl], 0))
        score_high, score_low = split(e_ref[head] * (inner - delta))
        both = jnp.concatenate([gh, gl], 0)
        value_part = product(eh_ref[head], both, True) + product(el_ref[head], both, True)
        both = jnp.concatenate([query_high[own], query_low[own]], 0)
        key_part = product(score_high, both, True) + product(score_low, both, True)
        if first:
            value_acc[head] = value_part
            key_acc[head] = key_part
        else:
            value_acc[head] += value_part
            key_acc[head] += key_part
        wide = product(kt_ref[head], score_high)
        through = wide[:HEAD_DIM] + wide[HEAD_DIM:] + product(kt_ref[head, :HEAD_DIM], score_low)
        parts.append(through * 0.125 + alpha * pooled + gamma * query)
    return jnp.concatenate(parts, 0).T


def folded(acc, out_ref, scale):
    patches = out_ref.shape[0]
    left = lax.broadcasted_iota(jnp.int32, (ROWS, 128), 1) < HEAD_DIM
    for pair in range(HEADS // 2):
        even, odd = acc[2 * pair], acc[2 * pair + 1]
        whole = jnp.where(left, even + pltpu.roll(even, HEAD_DIM, 1), odd + pltpu.roll(odd, HEAD_DIM, 1))
        out_ref[:, pair * 128:(pair + 1) * 128] = (whole * scale)[:patches]


def grads_kernel(first, last, chunk, *refs):
    q_ref, label_ref, kc_ref, vc_ref, kt_ref, vt_ref = refs[:6]
    refs = refs[6:]
    if not first:
        key_in, value_in = refs[:2]
        refs = refs[2:]
    dq_ref, dk_ref, dv_ref = refs[:3]
    if last:
        key_acc, value_acc = refs[3:5]
        scratch = refs[5:]
    else:
        key_acc, value_acc = dk_ref, dv_ref
        scratch = refs[3:]
    if not first:
        key_acc[...] = key_in[...]
        value_acc[...] = value_in[...]
    for start in range(0, q_ref.shape[0], chunk):
        part = slice(start, start + chunk)
        dq_ref[part, :] = chunk_grads(
            q_ref[part, :], label_ref[:, part], kc_ref, vc_ref, kt_ref, vt_ref,
            key_acc, value_acc, *scratch, first and start == 0)
    if last:
        folded(key_acc, dk_ref, LN2)
        folded(value_acc, dv_ref, 1.0)


def grads(q, label, prepared, acc=(), last=True, patches=196):
    rows = q.shape[0]
    chunk = min(rows, 256)
    acc_shape = (HEADS, ROWS, 128)
    big = jax.ShapeDtypeStruct((patches, 512) if last else acc_shape, jnp.float32)
    own_acc = [pltpu.VMEM(acc_shape, jnp.float32)] * 2 if last else []
    return pl.pallas_call(
        functools.partial(grads_kernel, not acc, last, chunk),
        out_shape=(jax.ShapeDtypeStruct((rows, 512), jnp.float32), big, big),
        scratch_shapes=own_acc + [
            pltpu.VMEM((HEADS, ROWS, chunk), jnp.float32),
            pltpu.VMEM((HEADS, ROWS, chunk), jnp.bfloat16),
            pltpu.VMEM((HEADS, ROWS, chunk), jnp.bfloat16),
            pltpu.VMEM((512, chunk), jnp.float32),
        ],
        name="grads",
    )(q, label, *prepared, *acc)


RING = ("y_hi", "x", "y_lo")


def spread(value, axis, count):
    return lax.all_to_all(jnp.broadcast_to(value[None], (count,) + value.shape), axis, 0, 0, tiled=True)


def swapped(value):
    return lax.ppermute(value, "core", [(0, 1), (1, 0)])


def per_device(patch_keys, patch_values, caption_queries, positive):
    sides = positive.reshape(8, 2, 32).swapaxes(0, 1).reshape(2, 1, 256)
    core = lax.axis_index("core")
    own_label = lax.dynamic_index_in_dim(sides, core, 0, keepdims=False)
    other_label = lax.dynamic_index_in_dim(sides, 1 - core, 0, keepdims=False)
    prepared = prepare(patch_keys[0], patch_values[0])
    row = spread(caption_queries, "z", 16).reshape(16, 512)
    own = spread(row, RING, 16).reshape(256, 512)
    other = swapped(own)
    dq_first, *acc = grads(own[:128], own_label[:, :128], prepared, last=False)
    dq_other, *acc = grads(other, other_label, prepared, acc, last=False)
    received = swapped(dq_other)
    dq_second, grad_keys, grad_values = grads(own[128:], own_label[:, 128:], prepared, acc)
    total = jnp.concatenate([dq_first, dq_second], 0) + received
    total = lax.all_to_all(total.reshape(16, 16, 512), RING, 0, 0, tiled=True).sum(0)
    total = lax.all_to_all(total.reshape(16, 1, 512), "z", 0, 0, tiled=True).sum(0)
    return grad_keys[None], grad_values[None], total


AXES = ("y_hi", "x", "core", "y_lo", "z")


def solution(mesh):
    fine = Mesh(mesh.devices.reshape(2, 4, 2, 2, 16), AXES)
    return jax.shard_map(
        per_device, mesh=fine,
        in_specs=(P(AXES, None, None), P(AXES, None, None), P(AXES, None), P(AXES, None)),
        out_specs=(P(AXES, None, None), P(AXES, None, None), P(AXES, None)),
        check_vma=False,
    )
```

time: 614 us -> 109 us (0.18)
  the two profiles are of different devices: /device:TPU:2 before, /device:TPU:8 now
where the time goes in v1:
time: 109 us; the launch traced here: 108 us
  blocking collectives  42.5 us (39%)
  Pallas kernels  21.8 us (20%)
  waiting for transfers between devices  16.5 us (15%)
  starting transfers between devices  15.3 us (14%)
  local copies, waits for them, and re-layouts  9.16 us (8%)
  other arithmetic  2.35 us (2%)
    all_to_all x1, blocking collectives, spread(): lax.all_to_all(jnp.broadcast_to(value[None], (count,) + value.shape), axi...  27.6 us
    pallas_call x3, Pallas kernels, grads(): pl.pallas_call(functools.partial(grads_kernel, not acc, last, chunk), out...  18.9 us
    all_to_all x1, blocking collectives, per_device(): lax.all_to_all(total.reshape(16, 16, 512), RING, 0, 0, tiled=True).sum(0)  14.9 us
    all_to_all x1, waiting for transfers between devices, per_device(): lax.all_to_all(total.reshape(16, 1, 512), 'z', 0, 0, tiled=True).sum(0)  10.2 us
    all_to_all x1, starting transfers between devices, spread(): lax.all_to_all(jnp.broadcast_to(value[None], (count,) + value.shape), axi...  7.52 us
    all_to_all x1, waiting for transfers between devices, spread(): lax.all_to_all(jnp.broadcast_to(value[None], (count,) + value.shape), axi...  6.28 us
    unnamed x19, local copies, waits for them, and re-layouts  4.78 us
    ppermute x2, starting transfers between devices, swapped(): return lax.ppermute(value, 'core', [(0, 1), (1, 0)])  4.31 us
  transfers between devices with their start and end apart: 4, of which 2 were waited for; matrix products, arithmetic and copies ran while one was open for 6% of the time, Pallas kernels for 14%

profile of v1, /device:TPU:8, one launch (start us, length us, event | category | flops | bytes accessed | tf_op | source)
XLA Modules:
  0.0 108.3 jit_solution(15805626315057101160)
XLA Ops:
  0.6 0.7 broadcast_in_dim.22
  1.3 27.6 %all_to_all.20 = f32[16,1,512]{2,1,0:T(1,128)S(1)} all-to-all(f32[16,1,512]{2,1,0:T(1,128)S(1)} %broadcast_in_dim.22), channel_id=1, replica_groups=mesh['y_hi'=2,'x'=4,'core'=2,'y_lo'=2,'z'=16] {'z'}, dimensions={0} | all-to-all | bytes 65536 | tf_op jit(solution)/shard_map/all_to_all | solution.py:180
  28.9 0.9 broadcast_in_dim.24
  29.8 7.5 %all-to-all-start.1 = ((f32[16,16,512]{2,1,0:T(8,128)}), f32[16,16,512]{2,1,0:T(8,128)S(1)}, u32[]{:S(2)}, u32[]{:S(2)}) async-start(f32[16,16,512]{2,1,0:T(8,128)} %broadcast_in_dim.24), calls=%async_computation.1 | async-start | bytes 1048576 | tf_op jit(solution)/shard_map/all_to_all | solution.py:180
  37.3 0.5 broadcast.4
  37.8 0.2 copy-done.6
  38.0 0.7 reduce.4
  38.6 0.1 reshape.28
  38.7 0.1 reshape.29
  38.8 1.0 copy_bitcast_fusion
  39.8 6.3 %all-to-all-done.1 = f32[16,16,512]{2,1,0:T(8,128)S(1)} async-done(((f32[16,16,512]{2,1,0:T(8,128)}), f32[16,16,512]{2,1,0:T(8,128)S(1)}, u32[]{:S(2)}, u32[]{:S(2)}) %all-to-all-start.1) | async-done | bytes 524320 | tf_op jit(solution)/shard_map/all_to_all | solution.py:180
  46.1 1.9 %collective-permute-start = (f32[256,512]{1,0:T(8,128)S(1)}, f32[256,512]{1,0:T(8,128)S(1)}, u32[]{:S(2)}, u32[]{:S(2)}) collective-permute-start(f32[256,512]{1,0:T(8,128)S(1)} %bitcast.23), channel_id=1, source_target_pairs={{0,32},{32,0},{1,33},{33,1},{2,34},{34,2},{3,35},{35,3},{4,36},{36... | collective-permute-start | bytes 1572872 | tf_op jit(solution)/shard_map/ppermute | solution.py:184
  48.0 0.6 dynamic-slice_bitcast_fusion
  48.5 3.0 %prepare.1 = (bf16[8,208,256]{2,1,0:T(8,128)(2,1)}, bf16[8,208,256]{2,1,0:T(8,128)(2,1)}, bf16[8,128,208]{2,1,0:T(8,128)(2,1)}, bf16[8,128,208]{2,1,0:T(8,128)(2,1)}) custom-call(f32[196,512]{1,0:T(8,128)} %get-tuple-element.45.k_ref, f32[196,512]{1,0:T(8,128)} %get-tuple-element.44.v_ref), custom_call_target="tpu_custom_call" | custom-call | tf_op jit(solution)/shard_map/prepare/pallas_call | solution.py:54
  51.5 0.6 fusion.1
  52.1 0.8 fusion
  52.9 6.2 %grads.3 = (f32[128,512]{1,0:T(8,128)}, f32[8,208,128]{2,1,0:T(8,128)}, f32[8,208,128]{2,1,0:T(8,128)}) custom-call(f32[128,512]{1,0:T(8,128)} %bitcast.25, s32[1,128]{1,0:T(1,128)} %get-tuple-element.42.refs_1_, bf16[8,208,256]{2,1,0:T(8,128)(2,1)} %get-tuple-element.16.refs_2_, bf16[8,208,256]{2,1,0:T(8,128)(2,1)} %get-tuple-element.17.refs_3_, ...), custom_call_target="tpu_custom_call" | custom-call | tf_op jit(solution)/shard_map/grads/pallas_call | solution.py:163
  59.2 0.0 collective-permute-done.refs_0_
  59.2 0.8 copy-done
  60.0 6.5 %grads.4 = (f32[256,512]{1,0:T(8,128)}, f32[8,208,128]{2,1,0:T(8,128)}, f32[8,208,128]{2,1,0:T(8,128)}) custom-call(f32[256,512]{1,0:T(8,128)} %copy-done, s32[1,256]{1,0:T(1,128)} %get-tuple-element.40.refs_1_, bf16[8,208,256]{2,1,0:T(8,128)(2,1)} %get-tuple-element.16.refs_2_, bf16[8,208,256]{2,1,0:T(8,128)(2,1)} %get-tuple-element.17.refs_3_, ...), custom_call_target="tpu_custom_call" | custom-call | tf_op jit(solution)/shard_map/grads/pallas_call | solution.py:163
  66.5 2.4 %collective-permute-start.1 = (f32[256,512]{1,0:T(8,128)}, f32[256,512]{1,0:T(8,128)S(1)}, u32[]{:S(2)}, u32[]{:S(2)}) collective-permute-start(f32[256,512]{1,0:T(8,128)} %get-tuple-element.28), channel_id=1, source_target_pairs={{0,32},{32,0},{1,33},{33,1},{2,34},{34,2},{3,35},{35,3},{4,36},{36... | collective-permute-start | bytes 1572872 | tf_op jit(solution)/shard_map/ppermute | solution.py:184
  68.9 6.1 %grads.5 = (f32[128,512]{1,0:T(8,128)}, f32[196,512]{1,0:T(8,128)}, f32[196,512]{1,0:T(8,128)}) custom-call(f32[128,512]{1,0:T(8,128)} %bitcast.24, s32[1,128]{1,0:T(1,128)} %get-tuple-element.43.refs_1_, bf16[8,208,256]{2,1,0:T(8,128)(2,1)} %get-tuple-element.16.refs_2_, bf16[8,208,256]{2,1,0:T(8,128)(2,1)} %get-tuple-element.17.refs_3_, ...), custom_call_target="tpu_custom_call" | custom-call | tf_op jit(solution)/shard_map/grads/pallas_call | solution.py:163
  75.0 0.0 collective-permute-done.1
  75.0 0.0 copy-done.5
  75.0 1.0 maximum_add_fusion
  76.1 14.9 %all_to_all.21 = f32[16,16,512]{2,1,0:T(8,128)S(1)} all-to-all(f32[16,16,512]{2,1,0:T(8,128)S(1)} %bitcast.22), channel_id=1, replica_groups=mesh['y_hi'=2,'x'=4,'core'=2,'y_lo'=2,'z'=16] {'y_hi','x','y_lo'}, dimensions={0} | all-to-all | bytes 1048576 | tf_op jit(solution)/shard_map/all_to_all | solution.py:201
  91.0 0.6 reshape.32
  91.7 3.5 %all-to-all-start.3 = ((f32[16,1,512]{2,1,0:T(1,128)}), f32[16,1,512]{2,1,0:T(1,128)S(1)}, u32[]{:S(2)}, u32[]{:S(2)}) async-start(f32[16,1,512]{2,1,0:T(1,128)} %reshape.32), calls=%async_computation.3 | async-start | bytes 65536 | tf_op jit(solution)/shard_map/all_to_all | solution.py:202
  95.2 1.2 %copy.13 = f32[1,196,512]{2,0,1:T(1,128)} copy(f32[1,196,512]{2,1,0:T(8,128)S(1)} %bitcast.27) | data formatting | bytes 802816
  96.3 1.2 %copy.14 = f32[1,196,512]{2,0,1:T(1,128)} copy(f32[1,196,512]{2,1,0:T(8,128)S(1)} %bitcast.26) | data formatting | bytes 802816
  97.5 10.2 %all-to-all-done.3 = f32[16,1,512]{2,1,0:T(1,128)S(1)} async-done(((f32[16,1,512]{2,1,0:T(1,128)}), f32[16,1,512]{2,1,0:T(1,128)S(1)}, u32[]{:S(2)}, u32[]{:S(2)}) %all-to-all-start.3) | async-done | bytes 32800 | tf_op jit(solution)/shard_map/all_to_all | solution.py:202
  107.7 0.6 reduce_sum.21
  (14 shorter events, 0.1 us)
Async XLA Ops:
  29.8 9.1 %copy-start.3 = (f32[1,196,512]{2,0,1:T(1,128)S(1)}, f32[1,196,512]{2,0,1:T(1,128)}, u32[]{:S(2)}) copy-start(f32[1,196,512]{2,0,1:T(1,128)} %param.5) | copy-start | bytes 1204228
  29.8 9.1 %copy-start.4 = (f32[1,196,512]{2,0,1:T(1,128)S(1)}, f32[1,196,512]{2,0,1:T(1,128)}, u32[]{:S(2)}) copy-start(f32[1,196,512]{2,0,1:T(1,128)} %param.4) | copy-start | bytes 1204228
  29.8 16.3 %all-to-all-start.1 = ((f32[16,16,512]{2,1,0:T(8,128)}), f32[16,16,512]{2,1,0:T(8,128)S(1)}, u32[]{:S(2)}, u32[]{:S(2)}) async-start(f32[16,16,512]{2,1,0:T(8,128)} %broadcast_in_dim.24), calls=%async_computation.1 | async-start | bytes 1048576 | tf_op jit(solution)/shard_map/all_to_all | solution.py:180
  37.3 0.7 copy-start.6
  46.1 13.1 %collective-permute-start = (f32[256,512]{1,0:T(8,128)S(1)}, f32[256,512]{1,0:T(8,128)S(1)}, u32[]{:S(2)}, u32[]{:S(2)}) collective-permute-start(f32[256,512]{1,0:T(8,128)S(1)} %bitcast.23), channel_id=1, source_target_pairs={{0,32},{32,0},{1,33},{33,1},{2,34},{34,2},{3,35},{35,3},{4,36},{36... | collective-permute-start | bytes 1572872 | tf_op jit(solution)/shard_map/ppermute | solution.py:184
  59.2 0.8 copy-start
  66.5 8.5 %collective-permute-start.1 = (f32[256,512]{1,0:T(8,128)}, f32[256,512]{1,0:T(8,128)S(1)}, u32[]{:S(2)}, u32[]{:S(2)}) collective-permute-start(f32[256,512]{1,0:T(8,128)} %get-tuple-element.28), channel_id=1, source_target_pairs={{0,32},{32,0},{1,33},{33,1},{2,34},{34,2},{3,35},{35,3},{4,36},{36... | collective-permute-start | bytes 1572872 | tf_op jit(solution)/shard_map/ppermute | solution.py:184
  68.9 6.1 %copy-start.5 = (f32[128,512]{1,0:T(8,128)S(1)}, f32[128,512]{1,0:T(8,128)}, u32[]{:S(2)}) copy-start(f32[128,512]{1,0:T(8,128)} %get-tuple-element.26) | copy-start | bytes 786436
  91.0 4.2 %copy-start.2 = (f32[196,512]{1,0:T(8,128)S(1)}, f32[196,512]{1,0:T(8,128)}, u32[]{:S(2)}) copy-start(f32[196,512]{1,0:T(8,128)} %get-tuple-element.24) | copy-start | bytes 1204228
  91.7 16.0 %all-to-all-start.3 = ((f32[16,1,512]{2,1,0:T(1,128)}), f32[16,1,512]{2,1,0:T(1,128)S(1)}, u32[]{:S(2)}, u32[]{:S(2)}) async-start(f32[16,1,512]{2,1,0:T(1,128)} %reshape.32), calls=%async_computation.3 | async-start | bytes 65536 | tf_op jit(solution)/shard_map/all_to_all | solution.py:202
  95.1 1.2 %copy-start.1 = (f32[196,512]{1,0:T(8,128)S(1)}, f32[196,512]{1,0:T(8,128)}, u32[]{:S(2)}) copy-start(f32[196,512]{1,0:T(8,128)} %get-tuple-element.25) | copy-start | bytes 1204228

commit v2 on v1

v2 whole, which is shorter than its diff:
```python
import math

import jax
import jax.numpy as jnp
from jax import lax
from jax.experimental import pallas as pl
from jax.experimental.pallas import tpu as pltpu
from jax.sharding import Mesh
from jax.sharding import PartitionSpec as P


HEADS = 8
HEAD_DIM = 64
PATCHES = 196
ROWS = 208
PART = 208
LOG2E = math.log2(math.e)
LN2 = math.log(2.0)
PARAMS = pltpu.CompilerParams(vmem_limit_bytes=24 * 1024 * 1024)


def split(x):
    high = x.astype(jnp.bfloat16)
    return high, (x - high.astype(jnp.float32)).astype(jnp.bfloat16)


def product(lhs, rhs, transposed=False):
    contract = ((1,), (1 if transposed else 0,))
    return lax.dot_general(lhs, rhs, (contract, ((), ())), preferred_element_type=jnp.float32)


def pack_kernel(k_ref, v_ref, label_ref, out_ref):
    out_ref[:PATCHES, :] = k_ref[:, 0, :]
    out_ref[PART:PART + PATCHES, :] = v_ref[:, 0, :]
    labels = jnp.broadcast_to(label_ref[...].astype(jnp.float32), (8, 512))
    out_ref[2 * PART - 8:, :] = labels


def pack(k, v, label):
    return pl.pallas_call(
        pack_kernel,
        out_shape=pltpu.VMEM((2 * PART, 512), jnp.float32),
        name="pack",
        compiler_params=PARAMS,
    )(k, v, label)


def prepare_kernel(packed_ref, kc_ref, vc_ref, kt_ref, vt_ref, label_ref, pad_ref):
    for start, cat_ref, turned_ref in ((0, kc_ref, kt_ref), (PART, vc_ref, vt_ref)):
        pad_ref[192:, :] = jnp.zeros((64, 512), jnp.float32)
        pad_ref[:PATCHES, :] = packed_ref[start:start + PATCHES, :]
        left = lax.broadcasted_iota(jnp.int32, (ROWS, 128), 1) < HEAD_DIM
        for pair in range(HEADS // 2):
            tile = pad_ref[:, pair * 128:(pair + 1) * 128]
            rows = tile[:ROWS]
            high = rows.astype(jnp.bfloat16).astype(jnp.float32)
            for place, part in ((0, high), (1, rows - high)):
                rolled = pltpu.roll(part, HEAD_DIM, 1)
                lanes = slice(place * 128, (place + 1) * 128)
                cat_ref[2 * pair, :, lanes] = jnp.where(left, part, rolled).astype(jnp.bfloat16)
                cat_ref[2 * pair + 1, :, lanes] = jnp.where(left, rolled, part).astype(jnp.bfloat16)
            turned_high, turned_low = split(tile.T)
            for side in range(2):
                own = slice(side * HEAD_DIM, (side + 1) * HEAD_DIM)
                turned_ref[2 * pair + side, :HEAD_DIM, :] = turned_high[own, :ROWS]
                turned_ref[2 * pair + side, HEAD_DIM:, :] = turned_low[own, :ROWS]
    label_ref[...] = packed_ref[2 * PART - 8:, :]


def prepare(packed):
    cat = pltpu.VMEM((HEADS, ROWS, 256), jnp.bfloat16)
    turned = pltpu.VMEM((HEADS, 128, ROWS), jnp.bfloat16)
    return pl.pallas_call(
        prepare_kernel,
        out_shape=(cat, cat, turned, turned, pltpu.VMEM((8, 512), jnp.float32)),
        scratch_shapes=[pltpu.VMEM((256, 512), jnp.float32)],
        name="prepare",
        compiler_params=PARAMS,
    )(*in_vmem(packed))


def folded(even, odd, scale, out_ref, start, lanes):
    left = lax.broadcasted_iota(jnp.int32, (ROWS, 128), 1) < HEAD_DIM
    whole = jnp.where(left, even + pltpu.roll(even, HEAD_DIM, 1), odd + pltpu.roll(odd, HEAD_DIM, 1))
    out_ref[start:start + ROWS, lanes] = whole * scale


def image_grads(turned, query_high, query_low, label, kc_ref, vc_ref, kt_ref, vt_ref, image_ref,
                e_ref, eh_ref, el_ref, o_ref):
    columns = turned.shape[1]
    inverse = []
    match = jnp.zeros((1, columns), jnp.float32)
    square = jnp.zeros((1, columns), jnp.float32)
    below = lax.broadcasted_iota(jnp.int32, (16, columns), 0) < 4
    for head in range(HEADS):
        own = slice(head * HEAD_DIM, (head + 1) * HEAD_DIM)
        qh, ql = query_high[own], query_low[own]
        scores = product(kc_ref[head], jnp.concatenate([qh, ql, qh, ql], 0))
        scores = jnp.concatenate([scores[:192], jnp.where(below, scores[192:], -1e30)], 0)
        exponent = jnp.exp2(scores - jnp.max(scores, axis=0, keepdims=True))
        inverse.append(1.0 / jnp.sum(exponent, axis=0, keepdims=True))
        high, low = split(exponent)
        e_ref[head] = exponent
        eh_ref[head] = high
        el_ref[head] = low
        wide = product(vt_ref[head], high)
        pooled = (wide[:HEAD_DIM] + wide[HEAD_DIM:] + product(vt_ref[head, :HEAD_DIM], low)) * inverse[head]
        o_ref[own, :] = pooled
        match += jnp.sum(pooled * turned[own], axis=0, keepdims=True)
        square += jnp.sum(pooled * pooled, axis=0, keepdims=True)
    width = HEADS * HEAD_DIM
    match = match / width
    summary = lax.rsqrt(square / width + 1e-6)
    probe = lax.rsqrt(jnp.sum(turned * turned, axis=0, keepdims=True) / width + 1e-6)
    sign = 2.0 * label - 1.0
    logit = 10.0 * match * summary * probe - 2.0
    slope = -sign / (1.0 + jnp.exp(sign * logit)) * (10.0 / width)
    alpha = slope * summary * probe
    beta = -alpha * match * summary * summary
    gamma = -alpha * match * probe * probe
    parts = []
    for head in range(HEADS):
        own = slice(head * HEAD_DIM, (head + 1) * HEAD_DIM)
        pooled = o_ref[own, :]
        query = turned[own]
        grad = (alpha * query + beta * pooled) * inverse[head]
        delta = jnp.sum(grad * pooled, axis=0, keepdims=True)
        gh, gl = split(grad)
        inner = product(vc_ref[head], jnp.concatenate([gh, gl, gh, gl], 0))
        score_high, score_low = split(e_ref[head] * (inner - delta))
        both = jnp.concatenate([gh, gl], 0)
        value_part = product(eh_ref[head], both, True) + product(el_ref[head], both, True)
        both = jnp.concatenate([query_high[own], query_low[own]], 0)
        key_part = product(score_high, both, True) + product(score_low, both, True)
        if head % 2 == 0:
            even = key_part, value_part
        else:
            lanes = slice((head - 1) * HEAD_DIM, (head + 1) * HEAD_DIM)
            folded(even[0], key_part, LN2, image_ref, 0, lanes)
            folded(even[1], value_part, 1.0, image_ref, PART, lanes)
        wide = product(kt_ref[head], score_high)
        through = wide[:HEAD_DIM] + wide[HEAD_DIM:] + product(kt_ref[head, :HEAD_DIM], score_low)
        parts.append(through * 0.125 + alpha * pooled + gamma * query)
    return jnp.concatenate(parts, 0)


def columns_of(label_ref, core):
    blocks = [label_ref[:1, start:start + 32] for start in range(0, 512, 32)]
    sides = [jnp.concatenate(blocks[side::2], 1) for side in range(2)]
    return jnp.where(core == 0, sides[0], sides[1])


def grads_kernel(core_ref, q_ref, *refs):
    images = (refs[:5], refs[5:10])
    dq_ref, *totals = refs[10:13]
    scratch = refs[13:]
    turned = q_ref[...].T
    query_high, query_low = split(turned * (LOG2E / 8.0))
    grad = 0.0
    for image in range(2):
        *arrays, label_ref = images[image]
        label = columns_of(label_ref, core_ref[0])
        grad += image_grads(turned, query_high, query_low, label, *arrays, totals[image], *scratch)
    dq_ref[...] = grad.T


def in_vmem(*values):
    return [pltpu.with_memory_space_constraint(value, pltpu.VMEM) for value in values]


def grads(core, q, own, other):
    chunk = q.shape[0]
    total = pltpu.VMEM((2 * PART, 512), jnp.float32)
    return pl.pallas_call(
        grads_kernel,
        in_specs=[pl.BlockSpec(memory_space=pltpu.SMEM)] + [pl.BlockSpec(memory_space=pltpu.VMEM)] * 11,
        out_shape=(pltpu.VMEM((chunk, 512), jnp.float32), total, total),
        scratch_shapes=[
            pltpu.VMEM((HEADS, ROWS, chunk), jnp.float32),
            pltpu.VMEM((HEADS, ROWS, chunk), jnp.bfloat16),
            pltpu.VMEM((HEADS, ROWS, chunk), jnp.bfloat16),
            pltpu.VMEM((512, chunk), jnp.float32),
        ],
        name="grads",
        compiler_params=PARAMS,
    )(core, *in_vmem(q, *own, *other))


def finish_kernel(own_ref, received_ref, dk_ref, dv_ref):
    for start, out_ref in ((0, dk_ref), (PART, dv_ref)):
        rows = slice(start, start + PATCHES)
        out_ref[:, 0, :] = own_ref[rows, :] + received_ref[rows, :]


def finish(own, received):
    out = jax.ShapeDtypeStruct((PATCHES, 1, 512), jnp.float32)
    return pl.pallas_call(
        finish_kernel, out_shape=(out, out), name="finish", compiler_params=PARAMS,
    )(*in_vmem(own, received))


RING = ("y_hi", "x", "y_lo")


def spread(value, axis, count):
    return lax.all_to_all(jnp.broadcast_to(value[None], (count,) + value.shape), axis, 0, 0, tiled=True)


def swapped(value):
    return lax.ppermute(value, "core", [(0, 1), (1, 0)])


def per_device(patch_keys, patch_values, caption_queries, positive):
    core = lax.axis_index("core").astype(jnp.int32).reshape(1)
    packed = pack(patch_keys.swapaxes(0, 1), patch_values.swapaxes(0, 1), positive)
    row = spread(caption_queries, "z", 16).reshape(16, 512)
    row, packed = lax.optimization_barrier((row, packed))
    queries = spread(row, RING, 16).reshape(256, 512)
    other = swapped(packed)
    queries, packed, other = lax.optimization_barrier((queries, packed, other))
    dq, own, foreign = grads(core, queries, prepare(packed), prepare(other))
    total = lax.all_to_all(dq.reshape(16, 16, 512), RING, 0, 0, tiled=True).sum(0)
    received = swapped(foreign)
    total = lax.all_to_all(total.reshape(16, 1, 512), "z", 0, 0, tiled=True).sum(0)
    grad_keys, grad_values = finish(own, received)
    return grad_keys.swapaxes(0, 1), grad_values.swapaxes(0, 1), total


AXES = ("y_hi", "x", "core", "y_lo", "z")


def solution(mesh):
    fine = Mesh(mesh.devices.reshape(2, 4, 2, 2, 16), AXES)
    return jax.shard_map(
        per_device, mesh=fine,
        in_specs=(P(AXES, None, None), P(AXES, None, None), P(AXES, None), P(AXES, None)),
        out_specs=(P(AXES, None, None), P(AXES, None, None), P(AXES, None)),
        check_vma=False,
    )
```

time: 109 us -> 93.6 us (0.86)
  Pallas kernels: 21.8 us -> 9.26 us
  blocking collectives: 42.5 us -> 30.5 us
  starting transfers between devices: 15.3 us -> 26.4 us
  local copies, waits for them, and re-layouts: 9.16 us -> 4.86 us
  waiting for transfers between devices: 16.5 us -> 20.7 us
  other arithmetic: 2.35 us -> 0.65 us
    all_to_all x1 -> x2, starting transfers between devices: 7.52 us -> 22.6 us  [spread(): lax.all_to_all(jnp.broadcast_to(value[None], (count,) + value.shape), axi...]
    all_to_all x1 -> x2, waiting for transfers between devices: 6.28 us -> 20.7 us  [spread(): lax.all_to_all(jnp.broadcast_to(value[None], (count,) + value.shape), axi...]
    pallas_call x4 -> x5, Pallas kernels: 21.8 us -> 9.26 us  [the longest x1 6.71 us: grads(): pl.pallas_call(grads_kernel, in_specs=[pl.BlockSpec(memory_space=pltpu.SM...]
    all_to_all x2, blocking collectives: 42.5 us -> 30.5 us  [the longest x1 15.4 us: per_device(): lax.all_to_all(dq.reshape(16, 16, 512), RING, 0, 0, tiled=True).sum(0)]
    all_to_all x1 -> x0, waiting for transfers between devices: 10.2 us -> none  [per_device(): lax.all_to_all(total.reshape(16, 1, 512), 'z', 0, 0, tiled=True).sum(0)]
    all_to_all x1 -> x0, starting transfers between devices: 3.47 us -> none  [per_device(): lax.all_to_all(total.reshape(16, 1, 512), 'z', 0, 0, tiled=True).sum(0)]
    unnamed x19 -> x7, local copies, waits for them, and re-layouts: 4.78 us -> 2.68 us
    slice x2 -> x0, local copies, waits for them, and re-layouts: 1.43 us -> none  [per_device(): dq_first, *acc = grads(own[:128], own_label[:, :128], prepared, last=False)]
  transfers between devices with their start and end apart: 4 -> 4, of which waited for: 2 -> 2; matrix products, arithmetic and copies ran while one was open for 6% -> 2% of each run, Pallas kernels for 14% -> 0%
where the time goes in v2:
time: 93.6 us; the launch traced here: 93.1 us
  blocking collectives  30.5 us (33%)
  starting transfers between devices  26.4 us (28%)
  waiting for transfers between devices  20.7 us (22%)
  Pallas kernels  9.26 us (10%)
  local copies, waits for them, and re-layouts  4.86 us (5%)
    all_to_all x2, starting transfers between devices, spread(): lax.all_to_all(jnp.broadcast_to(value[None], (count,) + value.shape), axi...  22.6 us
    all_to_all x2, waiting for transfers between devices, spread(): lax.all_to_all(jnp.broadcast_to(value[None], (count,) + value.shape), axi...  20.7 us
    all_to_all x1, blocking collectives, per_device(): lax.all_to_all(dq.reshape(16, 16, 512), RING, 0, 0, tiled=True).sum(0)  15.4 us
    all_to_all x1, blocking collectives, per_device(): lax.all_to_all(total.reshape(16, 1, 512), 'z', 0, 0, tiled=True).sum(0)  15.1 us
    pallas_call x1, Pallas kernels, grads(): pl.pallas_call(grads_kernel, in_specs=[pl.BlockSpec(memory_space=pltpu.SM...  6.71 us
    ppermute x2, starting transfers between devices, swapped(): return lax.ppermute(value, 'core', [(0, 1), (1, 0)])  3.83 us
    unnamed x7, local copies, waits for them, and re-layouts  2.68 us
    broadcast_in_dim x2, local copies, waits for them, and re-layouts, spread(): jnp.broadcast_to(value[None], (count,) + value.shape)  2.16 us
  transfers between devices with their start and end apart: 4, of which 2 were waited for; matrix products, arithmetic and copies ran while one was open for 2% of the time, Pallas kernels for 0%

profile of v2, /device:TPU:8, one launch (start us, length us, event | category | flops | bytes accessed | tf_op | source)
XLA Modules:
  0.0 93.1 jit_solution(1570264145277857637)
XLA Ops:
  0.6 1.3 %broadcast_in_dim.7 = f32[16,1,512]{2,1,0:T(1,128)} broadcast(f32[512]{0:T(512)} %bitcast.17), dimensions={2} | broadcast | bytes 34816 | tf_op jit(solution)/shard_map/broadcast_in_dim | solution.py:206
  1.9 15.2 %all-to-all-start = ((f32[16,1,512]{2,1,0:T(1,128)}), f32[16,1,512]{2,1,0:T(1,128)S(1)}, u32[]{:S(2)}, u32[]{:S(2)}) async-start(f32[16,1,512]{2,1,0:T(1,128)} %broadcast_in_dim.7), calls=%async_computation | async-start | bytes 65536 | tf_op jit(solution)/shard_map/all_to_all | solution.py:206
  17.1 0.0 copy-start.2
  17.2 0.7 copy-done.2
  17.8 0.0 copy-start
  17.8 1.0 %copy-done = f32[1,196,512]{2,0,1:T(1,128)S(1)} copy-done((f32[1,196,512]{2,0,1:T(1,128)S(1)}, f32[1,196,512]{2,0,1:T(1,128)}, u32[]{:S(2)}) %copy-start) | copy-done | bytes 401432
  18.8 0.0 copy-start.1
  18.8 1.0 %copy-done.1 = f32[1,196,512]{2,0,1:T(1,128)S(1)} copy-done((f32[1,196,512]{2,0,1:T(1,128)S(1)}, f32[1,196,512]{2,0,1:T(1,128)}, u32[]{:S(2)}) %copy-start.1) | copy-done | bytes 401432
  19.8 0.1 pack.1.packed_ref
  19.9 9.8 %all-to-all-done = f32[16,1,512]{2,1,0:T(1,128)S(1)} async-done(((f32[16,1,512]{2,1,0:T(1,128)}), f32[16,1,512]{2,1,0:T(1,128)S(1)}, u32[]{:S(2)}, u32[]{:S(2)}) %all-to-all-start) | async-done | bytes 32800 | tf_op jit(solution)/shard_map/all_to_all | solution.py:206
  29.7 1.9 %collective-permute-start = (f32[416,512]{1,0:T(8,128)S(1)}, f32[416,512]{1,0:T(8,128)S(1)}, u32[]{:S(2)}, u32[]{:S(2)}) collective-permute-start(f32[416,512]{1,0:T(8,128)S(1)} %pack.1.packed_ref), channel_id=1, source_target_pairs={{0,32},{32,0},{1,33},{33,1},{2,34},{34,2},{3,35},{35,3},{4,36},{36... | collective-permute-start | bytes 2555912 | tf_op jit(solution)/shard_map/ppermute | solution.py:210
  31.6 0.8 broadcast_in_dim.16
  32.5 7.4 %all-to-all-start.1 = ((f32[16,16,512]{2,1,0:T(8,128)}), f32[16,16,512]{2,1,0:T(8,128)S(1)}, u32[]{:S(2)}, u32[]{:S(2)}) async-start(f32[16,16,512]{2,1,0:T(8,128)} %broadcast_in_dim.16), calls=%async_computation.1 | async-start | bytes 1048576 | tf_op jit(solution)/shard_map/all_to_all | solution.py:206
  39.9 10.9 %all-to-all-done.1 = f32[16,16,512]{2,1,0:T(8,128)S(1)} async-done(((f32[16,16,512]{2,1,0:T(8,128)}), f32[16,16,512]{2,1,0:T(8,128)S(1)}, u32[]{:S(2)}, u32[]{:S(2)}) %all-to-all-start.1) | async-done | bytes 524320 | tf_op jit(solution)/shard_map/all_to_all | solution.py:206
  50.8 0.0 collective-permute-done.packed_ref
  50.8 0.7 prepare.2
  51.5 0.7 prepare.3
  52.3 6.7 %grads.1 = (f32[256,512]{1,0:T(8,128)S(1)}, f32[416,512]{1,0:T(8,128)S(1)}, f32[416,512]{1,0:T(8,128)S(1)}) custom-call(s32[1]{0:T(128)} %bitcast.core_ref, f32[256,512]{1,0:T(8,128)S(1)} %bitcast.12, bf16[8,208,256]{2,1,0:T(8,128)(2,1)S(1)} %get-tuple-element.27.refs_0_, bf16[8,208,256]{2,1,0:T(8,128)(2,1)S(1)} %get-tuple-element.28.refs_1_, ...), custom_call_target="tpu_custom_call" | custom-call | tf_op jit(solution)/shard_map/grads/pallas_call | solution.py:174
  59.0 1.9 %collective-permute-start.1 = (f32[416,512]{1,0:T(8,128)S(1)}, f32[416,512]{1,0:T(8,128)S(1)}, u32[]{:S(2)}, u32[]{:S(2)}) collective-permute-start(f32[416,512]{1,0:T(8,128)S(1)} %get-tuple-element.39), channel_id=1, source_target_pairs={{0,32},{32,0},{1,33},{33,1},{2,34},{34,2},{3,35},{35,3},{4,36},{36... | collective-permute-start | bytes 2555912 | tf_op jit(solution)/shard_map/ppermute | solution.py:210
  60.9 15.4 %all_to_all.20 = f32[16,16,512]{2,1,0:T(8,128)S(1)} all-to-all(f32[16,16,512]{2,1,0:T(8,128)S(1)} %bitcast.13), channel_id=1, replica_groups=mesh['y_hi'=2,'x'=4,'core'=2,'y_lo'=2,'z'=16] {'y_hi','x','y_lo'}, dimensions={0} | all-to-all | bytes 1048576 | tf_op jit(solution)/shard_map/all_to_all | solution.py:222
  76.4 15.1 %all_to_all.21 = f32[16,1,512]{2,1,0:T(1,128)S(1)} all-to-all(f32[16,1,512]{2,1,0:T(1,128)S(1)} %reshape.30), channel_id=1, replica_groups=mesh['y_hi'=2,'x'=4,'core'=2,'y_lo'=2,'z'=16] {'z'}, dimensions={0} | all-to-all | bytes 65536 | tf_op jit(solution)/shard_map/all_to_all | solution.py:224
  91.5 0.6 reduce_sum.21
  92.1 0.0 collective-permute-done.1.received_ref
  92.1 1.0 %finish.1 = (f32[196,1,512]{2,1,0:T(1,128)}, f32[196,1,512]{2,1,0:T(1,128)}) custom-call(f32[416,512]{1,0:T(8,128)S(1)} %get-tuple-element.38.own_ref, f32[416,512]{1,0:T(8,128)S(1)} %collective-permute-done.1.received_ref), custom_call_target="tpu_custom_call" | custom-call | tf_op jit(solution)/shard_map/finish/pallas_call | solution.py:197
  (3 shorter events, 0.1 us)
Async XLA Ops:
  1.9 27.8 %all-to-all-start = ((f32[16,1,512]{2,1,0:T(1,128)}), f32[16,1,512]{2,1,0:T(1,128)S(1)}, u32[]{:S(2)}, u32[]{:S(2)}) async-start(f32[16,1,512]{2,1,0:T(1,128)} %broadcast_in_dim.7), calls=%async_computation | async-start | bytes 65536 | tf_op jit(solution)/shard_map/all_to_all | solution.py:206
  17.1 0.7 copy-start.2
  17.8 1.0 %copy-start = (f32[1,196,512]{2,0,1:T(1,128)S(1)}, f32[1,196,512]{2,0,1:T(1,128)}, u32[]{:S(2)}) copy-start(f32[1,196,512]{2,0,1:T(1,128)} %param.4) | copy-start | bytes 1204228
  18.8 1.0 %copy-start.1 = (f32[1,196,512]{2,0,1:T(1,128)S(1)}, f32[1,196,512]{2,0,1:T(1,128)}, u32[]{:S(2)}) copy-start(f32[1,196,512]{2,0,1:T(1,128)} %param.5) | copy-start | bytes 1204228
  29.7 21.1 %collective-permute-start = (f32[416,512]{1,0:T(8,128)S(1)}, f32[416,512]{1,0:T(8,128)S(1)}, u32[]{:S(2)}, u32[]{:S(2)}) collective-permute-start(f32[416,512]{1,0:T(8,128)S(1)} %pack.1.packed_ref), channel_id=1, source_target_pairs={{0,32},{32,0},{1,33},{33,1},{2,34},{34,2},{3,35},{35,3},{4,36},{36... | collective-permute-start | bytes 2555912 | tf_op jit(solution)/shard_map/ppermute | solution.py:210
  32.5 18.3 %all-to-all-start.1 = ((f32[16,16,512]{2,1,0:T(8,128)}), f32[16,16,512]{2,1,0:T(8,128)S(1)}, u32[]{:S(2)}, u32[]{:S(2)}) async-start(f32[16,16,512]{2,1,0:T(8,128)} %broadcast_in_dim.16), calls=%async_computation.1 | async-start | bytes 1048576 | tf_op jit(solution)/shard_map/all_to_all | solution.py:206
  59.0 33.2 %collective-permute-start.1 = (f32[416,512]{1,0:T(8,128)S(1)}, f32[416,512]{1,0:T(8,128)S(1)}, u32[]{:S(2)}, u32[]{:S(2)}) collective-permute-start(f32[416,512]{1,0:T(8,128)S(1)} %get-tuple-element.39), channel_id=1, source_target_pairs={{0,32},{32,0},{1,33},{33,1},{2,34},{34,2},{3,35},{35,3},{4,36},{36... | collective-permute-start | bytes 2555912 | tf_op jit(solution)/shard_map/ppermute | solution.py:210

commit v3 on v2

--- a/solution.py
+++ b/solution.py
@@ -46,7 +46,7 @@
 
 
 def prepare_kernel(packed_ref, kc_ref, vc_ref, kt_ref, vt_ref, label_ref, pad_ref):
-    for start, cat_ref, turned_ref in ((0, kc_ref, kt_ref), (PART, vc_ref, vt_ref)):
+    for start, cat_ref, turned_ref, scale in ((0, kc_ref, kt_ref, 0.125), (PART, vc_ref, vt_ref, 1.0)):
         pad_ref[192:, :] = jnp.zeros((64, 512), jnp.float32)
         pad_ref[:PATCHES, :] = packed_ref[start:start + PATCHES, :]
         left = lax.broadcasted_iota(jnp.int32, (ROWS, 128), 1) < HEAD_DIM
@@ -59,7 +59,7 @@
                 lanes = slice(place * 128, (place + 1) * 128)
                 cat_ref[2 * pair, :, lanes] = jnp.where(left, part, rolled).astype(jnp.bfloat16)
                 cat_ref[2 * pair + 1, :, lanes] = jnp.where(left, rolled, part).astype(jnp.bfloat16)
-            turned_high, turned_low = split(tile.T)
+            turned_high, turned_low = split(tile.T * scale)
             for side in range(2):
                 own = slice(side * HEAD_DIM, (side + 1) * HEAD_DIM)
                 turned_ref[2 * pair + side, :HEAD_DIM, :] = turned_high[own, :ROWS]
@@ -79,69 +79,9 @@
     )(*in_vmem(packed))
 
 
-def folded(even, odd, scale, out_ref, start, lanes):
+def folded(even, odd):
     left = lax.broadcasted_iota(jnp.int32, (ROWS, 128), 1) < HEAD_DIM
-    whole = jnp.where(left, even + pltpu.roll(even, HEAD_DIM, 1), odd + pltpu.roll(odd, HEAD_DIM, 1))
-    out_ref[start:start + ROWS, lanes] = whole * scale
-
-
-def image_grads(turned, query_high, query_low, label, kc_ref, vc_ref, kt_ref, vt_ref, image_ref,
-                e_ref, eh_ref, el_ref, o_ref):
-    columns = turned.shape[1]
-    inverse = []
-    match = jnp.zeros((1, columns), jnp.float32)
-    square = jnp.zeros((1, columns), jnp.float32)
-    below = lax.broadcasted_iota(jnp.int32, (16, columns), 0) < 4
-    for head in range(HEADS):
-        own = slice(head * HEAD_DIM, (head + 1) * HEAD_DIM)
-        qh, ql = query_high[own], query_low[own]
-        scores = product(kc_ref[head], jnp.concatenate([qh, ql, qh, ql], 0))
-        scores = jnp.concatenate([scores[:192], jnp.where(below, scores[192:], -1e30)], 0)
-        exponent = jnp.exp2(scores - jnp.max(scores, axis=0, keepdims=True))
-        inverse.append(1.0 / jnp.sum(exponent, axis=0, keepdims=True))
-        high, low = split(exponent)
-        e_ref[head] = exponent
-        eh_ref[head] = high
-        el_ref[head] = low
-        wide = product(vt_ref[head], high)
-        pooled = (wide[:HEAD_DIM] + wide[HEAD_DIM:] + product(vt_ref[head, :HEAD_DIM], low)) * inverse[head]
-        o_ref[own, :] = pooled
-        match += jnp.sum(pooled * turned[own], axis=0, keepdims=True)
-        square += jnp.sum(pooled * pooled, axis=0, keepdims=True)
-    width = HEADS * HEAD_DIM
-    match = match / width
-    summary = lax.rsqrt(square / width + 1e-6)
-    probe = lax.rsqrt(jnp.sum(turned * turned, axis=0, keepdims=True) / width + 1e-6)
-    sign = 2.0 * label - 1.0
-    logit = 10.0 * match * summary * probe - 2.0
-    slope = -sign / (1.0 + jnp.exp(sign * logit)) * (10.0 / width)
-    alpha = slope * summary * probe
-    beta = -alpha * match * summary * summary
-    gamma = -alpha * match * probe * probe
-    parts = []
-    for head in range(HEADS):
-        own = slice(head * HEAD_DIM, (head + 1) * HEAD_DIM)
-        pooled = o_ref[own, :]
-        query = turned[own]
-        grad = (alpha * query + beta * pooled) * inverse[head]
-        delta = jnp.sum(grad * pooled, axis=0, keepdims=True)
-        gh, gl = split(grad)
-        inner = product(vc_ref[head], jnp.concatenate([gh, gl, gh, gl], 0))
-        score_high, score_low = split(e_ref[head] * (inner - delta))
-        both = jnp.concatenate([gh, gl], 0)
-        value_part = product(eh_ref[head], both, True) + product(el_ref[head], both, True)
-        both = jnp.concatenate([query_high[own], query_low[own]], 0)
-        key_part = product(score_high, both, True) + product(score_low, both, True)
-        if head % 2 == 0:
-            even = key_part, value_part
-        else:
-            lanes = slice((head - 1) * HEAD_DIM, (head + 1) * HEAD_DIM)
-            folded(even[0], key_part, LN2, image_ref, 0, lanes)
-            folded(even[1], value_part, 1.0, image_ref, PART, lanes)
-        wide = product(kt_ref[head], score_high)
-        through = wide[:HEAD_DIM] + wide[HEAD_DIM:] + product(kt_ref[head, :HEAD_DIM], score_low)
-        parts.append(through * 0.125 + alpha * pooled + gamma * query)
-    return jnp.concatenate(parts, 0)
+    return jnp.where(left, even + pltpu.roll(even, HEAD_DIM, 1), odd + pltpu.roll(odd, HEAD_DIM, 1))
 
 
 def columns_of(label_ref, core):
@@ -152,16 +92,85 @@
 
 def grads_kernel(core_ref, q_ref, *refs):
     images = (refs[:5], refs[5:10])
-    dq_ref, *totals = refs[10:13]
-    scratch = refs[13:]
+    dq_ref, *image_refs = refs[10:13]
+    e_ref, h_ref, o_ref, total_ref = refs[13:]
+    width = HEADS * HEAD_DIM
     turned = q_ref[...].T
+    columns = turned.shape[1]
+    probe = lax.rsqrt(jnp.sum(turned * turned, axis=0, keepdims=True) / width + 1e-6)
     query_high, query_low = split(turned * (LOG2E / 8.0))
-    grad = 0.0
-    for image in range(2):
-        *arrays, label_ref = images[image]
-        label = columns_of(label_ref, core_ref[0])
-        grad += image_grads(turned, query_high, query_low, label, *arrays, totals[image], *scratch)
-    dq_ref[...] = grad.T
+    below = lax.broadcasted_iota(jnp.int32, (16, columns), 0) < PATCHES - 192
+    inverse, match, square = ([[], []] for _ in range(3))
+
+    for head in range(HEADS):
+        own = slice(head * HEAD_DIM, (head + 1) * HEAD_DIM)
+        qh, ql = query_high[own], query_low[own]
+        keys = jnp.concatenate([images[0][0][head], images[1][0][head]], 0)
+        both = product(keys, jnp.concatenate([qh, ql, qh, ql], 0))
+        for place in range(2):
+            start = place * ROWS
+            scores = jnp.concatenate([
+                both[start:start + 192], jnp.where(below, both[start + 192:start + ROWS], -1e30)], 0)
+            exponent = jnp.exp2(scores - jnp.max(scores, axis=0, keepdims=True))
+            norm = 1.0 / jnp.sum(exponent, axis=0, keepdims=True)
+            high, low = split(exponent)
+            e_ref[head, start:start + ROWS, :] = exponent
+            h_ref[head, 2 * start:2 * start + ROWS, :] = high
+            h_ref[head, 2 * start + ROWS:2 * start + 2 * ROWS, :] = low
+            vt_ref = images[place][3]
+            wide = product(vt_ref[head], high)
+            pooled = (wide[:HEAD_DIM] + wide[HEAD_DIM:] + product(vt_ref[head, :HEAD_DIM], low)) * norm
+            o_ref[place, own, :] = pooled
+            inverse[place].append(norm)
+            match[place].append(jnp.sum(pooled * turned[own], axis=0, keepdims=True))
+            square[place].append(jnp.sum(pooled * pooled, axis=0, keepdims=True))
+
+    slopes = []
+    for place in range(2):
+        similar = sum(match[place]) / width
+        summary = lax.rsqrt(sum(square[place]) / width + 1e-6)
+        sign = 2.0 * columns_of(images[place][4], core_ref[0]) - 1.0
+        logit = 10.0 * similar * summary * probe - 2.0
+        slope = -sign / (1.0 + jnp.exp(sign * logit)) * (10.0 / width)
+        alpha = slope * summary * probe
+        slopes.append((alpha, -alpha * similar * summary * summary, -alpha * similar * probe * probe))
+    gamma = slopes[0][2] + slopes[1][2]
+
+    even = [None, None]
+    for head in range(HEADS):
+        own = slice(head * HEAD_DIM, (head + 1) * HEAD_DIM)
+        query = turned[own]
+        total = gamma * query
+        parts = []
+        value_parts = []
+        for place in range(2):
+            _, vc_ref, kt_ref, _, _ = images[place]
+            start = place * ROWS
+            alpha, beta, _ = slopes[place]
+            norm = inverse[place][head]
+            pooled = o_ref[place, own, :]
+            gh, gl = split((alpha * norm) * query + (beta * norm) * pooled)
+            delta = (alpha * match[place][head] + beta * square[place][head]) * norm
+            inner = product(vc_ref[head], jnp.concatenate([gh, gl, gh, gl], 0))
+            high, low = split(e_ref[head, start:start + ROWS, :] * (inner - delta))
+            parts += [high, low]
+            value = product(h_ref[head, 2 * start:2 * start + 2 * ROWS, :], jnp.concatenate([gh, gl], 0), True)
+            value_parts.append(value[:ROWS] + value[ROWS:])
+            wide = product(kt_ref[head], high)
+            total += wide[:HEAD_DIM] + wide[HEAD_DIM:] + product(kt_ref[head, :HEAD_DIM], low) + alpha * pooled
+        total_ref[own, :] = total
+        keys = product(
+            jnp.concatenate(parts, 0), jnp.concatenate([query_high[own], query_low[own]], 0), True)
+        for place in range(2):
+            start = 2 * place * ROWS
+            key = keys[start:start + ROWS] + keys[start + ROWS:start + 2 * ROWS]
+            if head % 2 == 0:
+                even[place] = key, value_parts[place]
+            else:
+                lanes = slice((head - 1) * HEAD_DIM, (head + 1) * HEAD_DIM)
+                image_refs[place][:ROWS, lanes] = folded(even[place][0], key) * LN2
+                image_refs[place][PART:, lanes] = folded(even[place][1], value_parts[place])
+    dq_ref[...] = total_ref[...].T
 
 
 def in_vmem(*values):
@@ -176,9 +185,9 @@
         in_specs=[pl.BlockSpec(memory_space=pltpu.SMEM)] + [pl.BlockSpec(memory_space=pltpu.VMEM)] * 11,
         out_shape=(pltpu.VMEM((chunk, 512), jnp.float32), total, total),
         scratch_shapes=[
-            pltpu.VMEM((HEADS, ROWS, chunk), jnp.float32),
-            pltpu.VMEM((HEADS, ROWS, chunk), jnp.bfloat16),
-            pltpu.VMEM((HEADS, ROWS, chunk), jnp.bfloat16),
+            pltpu.VMEM((HEADS, 2 * ROWS, chunk), jnp.float32),
+            pltpu.VMEM((HEADS, 4 * ROWS, chunk), jnp.bfloat16),
+            pltpu.VMEM((2, 512, chunk), jnp.float32),
             pltpu.VMEM((512, chunk), jnp.float32),
         ],
         name="grads",

time: 93.6 us -> 92.9 us (level)
  no operation moved by 1% of the time
where the time goes in v3:
time: 92.9 us; the launch traced here: 92.4 us
  blocking collectives  30.5 us (33%)
  starting transfers between devices  26.4 us (28%)
  waiting for transfers between devices  20.7 us (22%)
  Pallas kernels  8.55 us (9%)
  local copies, waits for them, and re-layouts  4.86 us (5%)
    all_to_all x2, starting transfers between devices, spread(): lax.all_to_all(jnp.broadcast_to(value[None], (count,) + value.shape), axi...  22.6 us
    all_to_all x2, waiting for transfers between devices, spread(): lax.all_to_all(jnp.broadcast_to(value[None], (count,) + value.shape), axi...  20.7 us
    all_to_all x1, blocking collectives, per_device(): lax.all_to_all(dq.reshape(16, 16, 512), RING, 0, 0, tiled=True).sum(0)  15.4 us
    all_to_all x1, blocking collectives, per_device(): lax.all_to_all(total.reshape(16, 1, 512), 'z', 0, 0, tiled=True).sum(0)  15.1 us
    pallas_call x1, Pallas kernels, grads(): pl.pallas_call(grads_kernel, in_specs=[pl.BlockSpec(memory_space=pltpu.SM...  5.99 us
    ppermute x2, starting transfers between devices, swapped(): return lax.ppermute(value, 'core', [(0, 1), (1, 0)])  3.83 us
    unnamed x7, local copies, waits for them, and re-layouts  2.68 us
    broadcast_in_dim x2, local copies, waits for them, and re-layouts, spread(): jnp.broadcast_to(value[None], (count,) + value.shape)  2.16 us
  transfers between devices with their start and end apart: 4, of which 2 were waited for; matrix products, arithmetic and copies ran while one was open for 2% of the time, Pallas kernels for 0%

profile of v3, /device:TPU:8, one launch (start us, length us, event | category | flops | bytes accessed | tf_op | source)
XLA Modules:
  0.0 92.4 jit_solution(9025390625192483150)
XLA Ops:
  0.6 1.3 %broadcast_in_dim.7 = f32[16,1,512]{2,1,0:T(1,128)} broadcast(f32[512]{0:T(512)} %bitcast.17), dimensions={2} | broadcast | bytes 34816 | tf_op jit(solution)/shard_map/broadcast_in_dim | solution.py:215
  1.9 15.2 %all-to-all-start = ((f32[16,1,512]{2,1,0:T(1,128)}), f32[16,1,512]{2,1,0:T(1,128)S(1)}, u32[]{:S(2)}, u32[]{:S(2)}) async-start(f32[16,1,512]{2,1,0:T(1,128)} %broadcast_in_dim.7), calls=%async_computation | async-start | bytes 65536 | tf_op jit(solution)/shard_map/all_to_all | solution.py:215
  17.1 0.0 copy-start.2
  17.2 0.7 copy-done.2
  17.8 0.0 copy-start
  17.8 1.0 %copy-done = f32[1,196,512]{2,0,1:T(1,128)S(1)} copy-done((f32[1,196,512]{2,0,1:T(1,128)S(1)}, f32[1,196,512]{2,0,1:T(1,128)}, u32[]{:S(2)}) %copy-start) | copy-done | bytes 401432
  18.8 0.0 copy-start.1
  18.8 1.0 %copy-done.1 = f32[1,196,512]{2,0,1:T(1,128)S(1)} copy-done((f32[1,196,512]{2,0,1:T(1,128)S(1)}, f32[1,196,512]{2,0,1:T(1,128)}, u32[]{:S(2)}) %copy-start.1) | copy-done | bytes 401432
  19.8 0.1 pack.1.packed_ref
  19.9 9.8 %all-to-all-done = f32[16,1,512]{2,1,0:T(1,128)S(1)} async-done(((f32[16,1,512]{2,1,0:T(1,128)}), f32[16,1,512]{2,1,0:T(1,128)S(1)}, u32[]{:S(2)}, u32[]{:S(2)}) %all-to-all-start) | async-done | bytes 32800 | tf_op jit(solution)/shard_map/all_to_all | solution.py:215
  29.7 1.9 %collective-permute-start = (f32[416,512]{1,0:T(8,128)S(1)}, f32[416,512]{1,0:T(8,128)S(1)}, u32[]{:S(2)}, u32[]{:S(2)}) collective-permute-start(f32[416,512]{1,0:T(8,128)S(1)} %pack.1.packed_ref), channel_id=1, source_target_pairs={{0,32},{32,0},{1,33},{33,1},{2,34},{34,2},{3,35},{35,3},{4,36},{36... | collective-permute-start | bytes 2555912 | tf_op jit(solution)/shard_map/ppermute | solution.py:219
  31.6 0.8 broadcast_in_dim.16
  32.5 7.4 %all-to-all-start.1 = ((f32[16,16,512]{2,1,0:T(8,128)}), f32[16,16,512]{2,1,0:T(8,128)S(1)}, u32[]{:S(2)}, u32[]{:S(2)}) async-start(f32[16,16,512]{2,1,0:T(8,128)} %broadcast_in_dim.16), calls=%async_computation.1 | async-start | bytes 1048576 | tf_op jit(solution)/shard_map/all_to_all | solution.py:215
  39.9 10.9 %all-to-all-done.1 = f32[16,16,512]{2,1,0:T(8,128)S(1)} async-done(((f32[16,16,512]{2,1,0:T(8,128)}), f32[16,16,512]{2,1,0:T(8,128)S(1)}, u32[]{:S(2)}, u32[]{:S(2)}) %all-to-all-start.1) | async-done | bytes 524320 | tf_op jit(solution)/shard_map/all_to_all | solution.py:215
  50.8 0.0 collective-permute-done.packed_ref
  50.8 0.7 prepare.2
  51.5 0.7 prepare.3
  52.3 6.0 %grads.1 = (f32[256,512]{1,0:T(8,128)S(1)}, f32[416,512]{1,0:T(8,128)S(1)}, f32[416,512]{1,0:T(8,128)S(1)}) custom-call(s32[1]{0:T(128)} %bitcast.core_ref, f32[256,512]{1,0:T(8,128)S(1)} %bitcast.12, bf16[8,208,256]{2,1,0:T(8,128)(2,1)S(1)} %get-tuple-element.27.refs_0_, bf16[8,208,256]{2,1,0:T(8,128)(2,1)S(1)} %get-tuple-element.28.refs_1_, ...), custom_call_target="tpu_custom_call" | custom-call | tf_op jit(solution)/shard_map/grads/pallas_call | solution.py:183
  58.3 1.9 %collective-permute-start.1 = (f32[416,512]{1,0:T(8,128)S(1)}, f32[416,512]{1,0:T(8,128)S(1)}, u32[]{:S(2)}, u32[]{:S(2)}) collective-permute-start(f32[416,512]{1,0:T(8,128)S(1)} %get-tuple-element.39), channel_id=1, source_target_pairs={{0,32},{32,0},{1,33},{33,1},{2,34},{34,2},{3,35},{35,3},{4,36},{36... | collective-permute-start | bytes 2555912 | tf_op jit(solution)/shard_map/ppermute | solution.py:219
  60.2 15.4 %all_to_all.20 = f32[16,16,512]{2,1,0:T(8,128)S(1)} all-to-all(f32[16,16,512]{2,1,0:T(8,128)S(1)} %bitcast.13), channel_id=1, replica_groups=mesh['y_hi'=2,'x'=4,'core'=2,'y_lo'=2,'z'=16] {'y_hi','x','y_lo'}, dimensions={0} | all-to-all | bytes 1048576 | tf_op jit(solution)/shard_map/all_to_all | solution.py:231
  75.7 15.1 %all_to_all.21 = f32[16,1,512]{2,1,0:T(1,128)S(1)} all-to-all(f32[16,1,512]{2,1,0:T(1,128)S(1)} %reshape.30), channel_id=1, replica_groups=mesh['y_hi'=2,'x'=4,'core'=2,'y_lo'=2,'z'=16] {'z'}, dimensions={0} | all-to-all | bytes 65536 | tf_op jit(solution)/shard_map/all_to_all | solution.py:233
  90.8 0.6 reduce_sum.21
  91.4 0.0 collective-permute-done.1.received_ref
  91.4 1.0 %finish.1 = (f32[196,1,512]{2,1,0:T(1,128)}, f32[196,1,512]{2,1,0:T(1,128)}) custom-call(f32[416,512]{1,0:T(8,128)S(1)} %get-tuple-element.38.own_ref, f32[416,512]{1,0:T(8,128)S(1)} %collective-permute-done.1.received_ref), custom_call_target="tpu_custom_call" | custom-call | tf_op jit(solution)/shard_map/finish/pallas_call | solution.py:206
  (3 shorter events, 0.1 us)
Async XLA Ops:
  1.9 27.8 %all-to-all-start = ((f32[16,1,512]{2,1,0:T(1,128)}), f32[16,1,512]{2,1,0:T(1,128)S(1)}, u32[]{:S(2)}, u32[]{:S(2)}) async-start(f32[16,1,512]{2,1,0:T(1,128)} %broadcast_in_dim.7), calls=%async_computation | async-start | bytes 65536 | tf_op jit(solution)/shard_map/all_to_all | solution.py:215
  17.1 0.7 copy-start.2
  17.8 1.0 %copy-start = (f32[1,196,512]{2,0,1:T(1,128)S(1)}, f32[1,196,512]{2,0,1:T(1,128)}, u32[]{:S(2)}) copy-start(f32[1,196,512]{2,0,1:T(1,128)} %param.4) | copy-start | bytes 1204228
  18.8 1.0 %copy-start.1 = (f32[1,196,512]{2,0,1:T(1,128)S(1)}, f32[1,196,512]{2,0,1:T(1,128)}, u32[]{:S(2)}) copy-start(f32[1,196,512]{2,0,1:T(1,128)} %param.5) | copy-start | bytes 1204228
  29.7 21.1 %collective-permute-start = (f32[416,512]{1,0:T(8,128)S(1)}, f32[416,512]{1,0:T(8,128)S(1)}, u32[]{:S(2)}, u32[]{:S(2)}) collective-permute-start(f32[416,512]{1,0:T(8,128)S(1)} %pack.1.packed_ref), channel_id=1, source_target_pairs={{0,32},{32,0},{1,33},{33,1},{2,34},{34,2},{3,35},{35,3},{4,36},{36... | collective-permute-start | bytes 2555912 | tf_op jit(solution)/shard_map/ppermute | solution.py:219
  32.5 18.3 %all-to-all-start.1 = ((f32[16,16,512]{2,1,0:T(8,128)}), f32[16,16,512]{2,1,0:T(8,128)S(1)}, u32[]{:S(2)}, u32[]{:S(2)}) async-start(f32[16,16,512]{2,1,0:T(8,128)} %broadcast_in_dim.16), calls=%async_computation.1 | async-start | bytes 1048576 | tf_op jit(solution)/shard_map/all_to_all | solution.py:215
  58.3 33.2 %collective-permute-start.1 = (f32[416,512]{1,0:T(8,128)S(1)}, f32[416,512]{1,0:T(8,128)S(1)}, u32[]{:S(2)}, u32[]{:S(2)}) collective-permute-start(f32[416,512]{1,0:T(8,128)S(1)} %get-tuple-element.39), channel_id=1, source_target_pairs={{0,32},{32,0},{1,33},{33,1},{2,34},{34,2},{3,35},{35,3},{4,36},{36... | collective-permute-start | bytes 2555912 | tf_op jit(solution)/shard_map/ppermute | solution.py:219

commit v4 on v3

--- a/solution.py
+++ b/solution.py
@@ -45,11 +45,11 @@
     )(k, v, label)
 
 
-def prepare_kernel(packed_ref, kc_ref, vc_ref, kt_ref, vt_ref, label_ref, pad_ref):
+def prepare_image(packed_ref, kc_ref, vc_ref, kt_ref, vt_ref, pad_ref):
+    left = lax.broadcasted_iota(jnp.int32, (ROWS, 128), 1) < HEAD_DIM
     for start, cat_ref, turned_ref, scale in ((0, kc_ref, kt_ref, 0.125), (PART, vc_ref, vt_ref, 1.0)):
         pad_ref[192:, :] = jnp.zeros((64, 512), jnp.float32)
         pad_ref[:PATCHES, :] = packed_ref[start:start + PATCHES, :]
-        left = lax.broadcasted_iota(jnp.int32, (ROWS, 128), 1) < HEAD_DIM
         for pair in range(HEADS // 2):
             tile = pad_ref[:, pair * 128:(pair + 1) * 128]
             rows = tile[:ROWS]
@@ -64,19 +64,6 @@
                 own = slice(side * HEAD_DIM, (side + 1) * HEAD_DIM)
                 turned_ref[2 * pair + side, :HEAD_DIM, :] = turned_high[own, :ROWS]
                 turned_ref[2 * pair + side, HEAD_DIM:, :] = turned_low[own, :ROWS]
-    label_ref[...] = packed_ref[2 * PART - 8:, :]
-
-
-def prepare(packed):
-    cat = pltpu.VMEM((HEADS, ROWS, 256), jnp.bfloat16)
-    turned = pltpu.VMEM((HEADS, 128, ROWS), jnp.bfloat16)
-    return pl.pallas_call(
-        prepare_kernel,
-        out_shape=(cat, cat, turned, turned, pltpu.VMEM((8, 512), jnp.float32)),
-        scratch_shapes=[pltpu.VMEM((256, 512), jnp.float32)],
-        name="prepare",
-        compiler_params=PARAMS,
-    )(*in_vmem(packed))
 
 
 def folded(even, odd):
@@ -91,9 +78,15 @@
 
 
 def grads_kernel(core_ref, q_ref, *refs):
-    images = (refs[:5], refs[5:10])
-    dq_ref, *image_refs = refs[10:13]
-    e_ref, h_ref, o_ref, total_ref = refs[13:]
+    packed = refs[:2]
+    dq_ref, own_ref, foreign_ref = refs[2:5]
+    e_ref, h_ref, o_ref, tile_ref, sems, image_ref, image_sems = refs[5:12]
+    image_refs = image_ref, foreign_ref
+    images = []
+    for place in range(2):
+        arrays = refs[12 + 5 * place:17 + 5 * place]
+        prepare_image(packed[place], *arrays)
+        images.append((*arrays[:4], packed[place].at[2 * PART - 8:, :]))
     width = HEADS * HEAD_DIM
     turned = q_ref[...].T
     columns = turned.shape[1]
@@ -137,6 +130,8 @@
     gamma = slopes[0][2] + slopes[1][2]
 
     even = [None, None]
+    parts_of_pair = []
+    copies = []
     for head in range(HEADS):
         own = slice(head * HEAD_DIM, (head + 1) * HEAD_DIM)
         query = turned[own]
@@ -158,9 +153,16 @@
             value_parts.append(value[:ROWS] + value[ROWS:])
             wide = product(kt_ref[head], high)
             total += wide[:HEAD_DIM] + wide[HEAD_DIM:] + product(kt_ref[head, :HEAD_DIM], low) + alpha * pooled
-        total_ref[own, :] = total
+        parts_of_pair.append(total)
         keys = product(
             jnp.concatenate(parts, 0), jnp.concatenate([query_high[own], query_low[own]], 0), True)
+        if head % 2 == 1:
+            pair = head // 2
+            lanes = slice(pair * 128, (pair + 1) * 128)
+            tile_ref[:, lanes] = jnp.concatenate(parts_of_pair, 0).T
+            parts_of_pair = []
+            copies.append(pltpu.make_async_copy(tile_ref.at[:, lanes], dq_ref.at[:, lanes], sems.at[pair]))
+            copies[-1].start()
         for place in range(2):
             start = 2 * place * ROWS
             key = keys[start:start + ROWS] + keys[start + ROWS:start + 2 * ROWS]
@@ -170,7 +172,11 @@
                 lanes = slice((head - 1) * HEAD_DIM, (head + 1) * HEAD_DIM)
                 image_refs[place][:ROWS, lanes] = folded(even[place][0], key) * LN2
                 image_refs[place][PART:, lanes] = folded(even[place][1], value_parts[place])
-    dq_ref[...] = total_ref[...].T
+        if head % 2 == 1:
+            copies.append(pltpu.make_async_copy(image_ref.at[:, lanes], own_ref.at[:, lanes], image_sems.at[pair]))
+            copies[-1].start()
+    for copy in copies:
+        copy.wait()
 
 
 def in_vmem(*values):
@@ -180,19 +186,27 @@
 def grads(core, q, own, other):
     chunk = q.shape[0]
     total = pltpu.VMEM((2 * PART, 512), jnp.float32)
+    cat = pltpu.VMEM((HEADS, ROWS, 256), jnp.bfloat16)
+    turned = pltpu.VMEM((HEADS, 128, ROWS), jnp.bfloat16)
+    vmem = pl.BlockSpec(memory_space=pltpu.VMEM)
+    hbm = pl.BlockSpec(memory_space=pltpu.HBM)
     return pl.pallas_call(
         grads_kernel,
-        in_specs=[pl.BlockSpec(memory_space=pltpu.SMEM)] + [pl.BlockSpec(memory_space=pltpu.VMEM)] * 11,
-        out_shape=(pltpu.VMEM((chunk, 512), jnp.float32), total, total),
+        in_specs=[pl.BlockSpec(memory_space=pltpu.SMEM)] + [vmem] * 3,
+        out_specs=(hbm, hbm, vmem),
+        out_shape=(pltpu.HBM((chunk, 512), jnp.float32), pltpu.HBM((2 * PART, 512), jnp.float32), total),
         scratch_shapes=[
             pltpu.VMEM((HEADS, 2 * ROWS, chunk), jnp.float32),
             pltpu.VMEM((HEADS, 4 * ROWS, chunk), jnp.bfloat16),
             pltpu.VMEM((2, 512, chunk), jnp.float32),
-            pltpu.VMEM((512, chunk), jnp.float32),
-        ],
+            pltpu.VMEM((chunk, 512), jnp.float32),
+            pltpu.SemaphoreType.DMA((HEADS // 2,)),
+            pltpu.VMEM((2 * PART, 512), jnp.float32),
+            pltpu.SemaphoreType.DMA((HEADS // 2,)),
+        ] + [cat, cat, turned, turned, pltpu.VMEM((256, 512), jnp.float32)] * 2,
         name="grads",
         compiler_params=PARAMS,
-    )(core, *in_vmem(q, *own, *other))
+    )(core, *in_vmem(q, own, other))
 
 
 def finish_kernel(own_ref, received_ref, dk_ref, dv_ref):
@@ -227,7 +241,7 @@
     queries = spread(row, RING, 16).reshape(256, 512)
     other = swapped(packed)
     queries, packed, other = lax.optimization_barrier((queries, packed, other))
-    dq, own, foreign = grads(core, queries, prepare(packed), prepare(other))
+    dq, own, foreign = grads(core, queries, packed, other)
     total = lax.all_to_all(dq.reshape(16, 16, 512), RING, 0, 0, tiled=True).sum(0)
     received = swapped(foreign)
     total = lax.all_to_all(total.reshape(16, 1, 512), "z", 0, 0, tiled=True).sum(0)

time: 92.9 us -> 94 us (1.012)
  blocking collectives: 30.5 us -> 31.5 us
    pallas_call x1, Pallas kernels: 5.99 us -> 7.5 us  [grads(): pl.pallas_call(grads_kernel, in_specs=[pl.BlockSpec(memory_space=pltpu.SM...]
    pallas_call x2 -> x0, Pallas kernels: 1.48 us -> none  [prepare(): pl.pallas_call(prepare_kernel, out_shape=(cat, cat, turned, turned, pltpu...]
    unnamed x7 -> x9, local copies, waits for them, and re-layouts: 2.68 us -> 2.68 us
where the time goes in v4:
time: 94 us; the launch traced here: 93.4 us
  blocking collectives  31.5 us (34%)
  starting transfers between devices  26.4 us (28%)
  waiting for transfers between devices  20.7 us (22%)
  Pallas kernels  8.58 us (9%)
  local copies, waits for them, and re-layouts  4.87 us (5%)
    all_to_all x2, starting transfers between devices, spread(): lax.all_to_all(jnp.broadcast_to(value[None], (count,) + value.shape), axi...  22.6 us
    all_to_all x2, waiting for transfers between devices, spread(): lax.all_to_all(jnp.broadcast_to(value[None], (count,) + value.shape), axi...  20.7 us
    all_to_all x1, blocking collectives, per_device(): lax.all_to_all(dq.reshape(16, 16, 512), RING, 0, 0, tiled=True).sum(0)  16.3 us
    all_to_all x1, blocking collectives, per_device(): lax.all_to_all(total.reshape(16, 1, 512), 'z', 0, 0, tiled=True).sum(0)  15.1 us
    pallas_call x1, Pallas kernels, grads(): pl.pallas_call(grads_kernel, in_specs=[pl.BlockSpec(memory_space=pltpu.SM...  7.5 us
    ppermute x2, starting transfers between devices, swapped(): return lax.ppermute(value, 'core', [(0, 1), (1, 0)])  3.83 us
    unnamed x9, local copies, waits for them, and re-layouts  2.68 us
    broadcast_in_dim x2, local copies, waits for them, and re-layouts, spread(): jnp.broadcast_to(value[None], (count,) + value.shape)  2.17 us
  transfers between devices with their start and end apart: 4, of which 2 were waited for; matrix products, arithmetic and copies ran while one was open for 2% of the time, Pallas kernels for 0%

profile of v4, /device:TPU:8, one launch (start us, length us, event | category | flops | bytes accessed | tf_op | source)
XLA Modules:
  0.0 93.4 jit_solution(3197643643883967803)
XLA Ops:
  0.6 1.3 %broadcast_in_dim.7 = f32[16,1,512]{2,1,0:T(1,128)} broadcast(f32[512]{0:T(512)} %bitcast.17), dimensions={2} | broadcast | bytes 34816 | tf_op jit(solution)/shard_map/broadcast_in_dim | solution.py:229
  1.9 15.2 %all-to-all-start = ((f32[16,1,512]{2,1,0:T(1,128)}), f32[16,1,512]{2,1,0:T(1,128)S(1)}, u32[]{:S(2)}, u32[]{:S(2)}) async-start(f32[16,1,512]{2,1,0:T(1,128)} %broadcast_in_dim.7), calls=%async_computation | async-start | bytes 65536 | tf_op jit(solution)/shard_map/all_to_all | solution.py:229
  17.1 0.0 copy-start.3
  17.2 0.7 copy-done.3
  17.8 0.0 copy-start.1
  17.8 1.0 %copy-done.1 = f32[1,196,512]{2,0,1:T(1,128)S(1)} copy-done((f32[1,196,512]{2,0,1:T(1,128)S(1)}, f32[1,196,512]{2,0,1:T(1,128)}, u32[]{:S(2)}) %copy-start.1) | copy-done | bytes 401432
  18.8 0.0 copy-start.2
  18.8 1.0 %copy-done.2 = f32[1,196,512]{2,0,1:T(1,128)S(1)} copy-done((f32[1,196,512]{2,0,1:T(1,128)S(1)}, f32[1,196,512]{2,0,1:T(1,128)}, u32[]{:S(2)}) %copy-start.2) | copy-done | bytes 401432
  19.8 0.1 pack.1.refs_0_
  19.9 9.8 %all-to-all-done = f32[16,1,512]{2,1,0:T(1,128)S(1)} async-done(((f32[16,1,512]{2,1,0:T(1,128)}), f32[16,1,512]{2,1,0:T(1,128)S(1)}, u32[]{:S(2)}, u32[]{:S(2)}) %all-to-all-start) | async-done | bytes 32800 | tf_op jit(solution)/shard_map/all_to_all | solution.py:229
  29.7 1.9 %collective-permute-start = (f32[416,512]{1,0:T(8,128)S(1)}, f32[416,512]{1,0:T(8,128)S(1)}, u32[]{:S(2)}, u32[]{:S(2)}) collective-permute-start(f32[416,512]{1,0:T(8,128)S(1)} %pack.1.refs_0_), channel_id=1, source_target_pairs={{0,32},{32,0},{1,33},{33,1},{2,34},{34,2},{3,35},{35,3},{4,36},{36... | collective-permute-start | bytes 2555912 | tf_op jit(solution)/shard_map/ppermute | solution.py:233
  31.6 0.9 broadcast_in_dim.16
  32.5 7.4 %all-to-all-start.1 = ((f32[16,16,512]{2,1,0:T(8,128)}), f32[16,16,512]{2,1,0:T(8,128)S(1)}, u32[]{:S(2)}, u32[]{:S(2)}) async-start(f32[16,16,512]{2,1,0:T(8,128)} %broadcast_in_dim.16), calls=%async_computation.1 | async-start | bytes 1048576 | tf_op jit(solution)/shard_map/all_to_all | solution.py:229
  39.9 10.9 %all-to-all-done.1 = f32[16,16,512]{2,1,0:T(8,128)S(1)} async-done(((f32[16,16,512]{2,1,0:T(8,128)}), f32[16,16,512]{2,1,0:T(8,128)S(1)}, u32[]{:S(2)}, u32[]{:S(2)}) %all-to-all-start.1) | async-done | bytes 524320 | tf_op jit(solution)/shard_map/all_to_all | solution.py:229
  50.8 0.0 collective-permute-done.refs_1_
  50.8 7.5 %grads.1 = (f32[256,512]{1,0:T(8,128)}, f32[416,512]{1,0:T(8,128)}, f32[416,512]{1,0:T(8,128)S(1)}) custom-call(s32[1]{0:T(128)} %bitcast.core_ref, f32[256,512]{1,0:T(8,128)S(1)} %bitcast.12, f32[416,512]{1,0:T(8,128)S(1)} %pack.1.refs_0_, f32[416,512]{1,0:T(8,128)S(1)} %collective-permute-done.refs_1_), custom_call_target="tpu_custom_call" | custom-call | tf_op jit(solution)/shard_map/grads/pallas_call | solution.py:193
  58.3 1.9 %collective-permute-start.1 = (f32[416,512]{1,0:T(8,128)S(1)}, f32[416,512]{1,0:T(8,128)S(1)}, u32[]{:S(2)}, u32[]{:S(2)}) collective-permute-start(f32[416,512]{1,0:T(8,128)S(1)} %get-tuple-element.19), channel_id=1, source_target_pairs={{0,32},{32,0},{1,33},{33,1},{2,34},{34,2},{3,35},{35,3},{4,36},{36... | collective-permute-start | bytes 2555912 | tf_op jit(solution)/shard_map/ppermute | solution.py:233
  60.2 0.0 copy-start
  60.2 16.3 %all_to_all.20 = f32[16,16,512]{2,1,0:T(8,128)S(1)} all-to-all(f32[16,16,512]{2,1,0:T(8,128)} %bitcast.15), channel_id=1, replica_groups=mesh['y_hi'=2,'x'=4,'core'=2,'y_lo'=2,'z'=16] {'y_hi','x','y_lo'}, dimensions={0} | all-to-all | bytes 1048576 | tf_op jit(solution)/shard_map/all_to_all | solution.py:245
  76.6 15.1 %all_to_all.21 = f32[16,1,512]{2,1,0:T(1,128)S(1)} all-to-all(f32[16,1,512]{2,1,0:T(1,128)S(1)} %reshape.30), channel_id=1, replica_groups=mesh['y_hi'=2,'x'=4,'core'=2,'y_lo'=2,'z'=16] {'z'}, dimensions={0} | all-to-all | bytes 65536 | tf_op jit(solution)/shard_map/all_to_all | solution.py:247
  91.8 0.6 reduce_sum.21
  92.4 0.0 collective-permute-done.1.received_ref
  92.4 0.0 copy-done
  92.4 1.0 %finish.1 = (f32[196,1,512]{2,1,0:T(1,128)}, f32[196,1,512]{2,1,0:T(1,128)}) custom-call(f32[416,512]{1,0:T(8,128)S(1)} %copy-done, f32[416,512]{1,0:T(8,128)S(1)} %collective-permute-done.1.received_ref), custom_call_target="tpu_custom_call" | custom-call | tf_op jit(solution)/shard_map/finish/pallas_call | solution.py:220
  (3 shorter events, 0.1 us)
Async XLA Ops:
  1.9 27.8 %all-to-all-start = ((f32[16,1,512]{2,1,0:T(1,128)}), f32[16,1,512]{2,1,0:T(1,128)S(1)}, u32[]{:S(2)}, u32[]{:S(2)}) async-start(f32[16,1,512]{2,1,0:T(1,128)} %broadcast_in_dim.7), calls=%async_computation | async-start | bytes 65536 | tf_op jit(solution)/shard_map/all_to_all | solution.py:229
  17.1 0.7 copy-start.3
  17.8 1.0 %copy-start.1 = (f32[1,196,512]{2,0,1:T(1,128)S(1)}, f32[1,196,512]{2,0,1:T(1,128)}, u32[]{:S(2)}) copy-start(f32[1,196,512]{2,0,1:T(1,128)} %param.4) | copy-start | bytes 1204228
  18.8 1.0 %copy-start.2 = (f32[1,196,512]{2,0,1:T(1,128)S(1)}, f32[1,196,512]{2,0,1:T(1,128)}, u32[]{:S(2)}) copy-start(f32[1,196,512]{2,0,1:T(1,128)} %param.5) | copy-start | bytes 1204228
  29.7 21.1 %collective-permute-start = (f32[416,512]{1,0:T(8,128)S(1)}, f32[416,512]{1,0:T(8,128)S(1)}, u32[]{:S(2)}, u32[]{:S(2)}) collective-permute-start(f32[416,512]{1,0:T(8,128)S(1)} %pack.1.refs_0_), channel_id=1, source_target_pairs={{0,32},{32,0},{1,33},{33,1},{2,34},{34,2},{3,35},{35,3},{4,36},{36... | collective-permute-start | bytes 2555912 | tf_op jit(solution)/shard_map/ppermute | solution.py:233
  32.5 18.3 %all-to-all-start.1 = ((f32[16,16,512]{2,1,0:T(8,128)}), f32[16,16,512]{2,1,0:T(8,128)S(1)}, u32[]{:S(2)}, u32[]{:S(2)}) async-start(f32[16,16,512]{2,1,0:T(8,128)} %broadcast_in_dim.16), calls=%async_computation.1 | async-start | bytes 1048576 | tf_op jit(solution)/shard_map/all_to_all | solution.py:229
  58.3 34.1 %collective-permute-start.1 = (f32[416,512]{1,0:T(8,128)S(1)}, f32[416,512]{1,0:T(8,128)S(1)}, u32[]{:S(2)}, u32[]{:S(2)}) collective-permute-start(f32[416,512]{1,0:T(8,128)S(1)} %get-tuple-element.19), channel_id=1, source_target_pairs={{0,32},{32,0},{1,33},{33,1},{2,34},{34,2},{3,35},{35,3},{4,36},{36... | collective-permute-start | bytes 2555912 | tf_op jit(solution)/shard_map/ppermute | solution.py:233
  60.2 32.2 %copy-start = (f32[416,512]{1,0:T(8,128)S(1)}, f32[416,512]{1,0:T(8,128)}, u32[]{:S(2)}) copy-start(f32[416,512]{1,0:T(8,128)} %get-tuple-element.18.own_ref) | copy-start | bytes 2555908

commit v5 on v4

--- a/solution.py
+++ b/solution.py
@@ -29,20 +29,36 @@
     return lax.dot_general(lhs, rhs, (contract, ((), ())), preferred_element_type=jnp.float32)
 
 
-def pack_kernel(k_ref, v_ref, label_ref, out_ref):
-    out_ref[:PATCHES, :] = k_ref[:, 0, :]
-    out_ref[PART:PART + PATCHES, :] = v_ref[:, 0, :]
-    labels = jnp.broadcast_to(label_ref[...].astype(jnp.float32), (8, 512))
-    out_ref[2 * PART - 8:, :] = labels
+def pack_kernel(k_ref, v_ref, label_ref, out_ref, rows_ref, row_ref, sems):
+    copies = [
+        pltpu.make_async_copy(k_ref, rows_ref.at[0], sems.at[0]),
+        pltpu.make_async_copy(v_ref, rows_ref.at[1], sems.at[1]),
+        pltpu.make_async_copy(label_ref, row_ref, sems.at[2]),
+    ]
+    for copy in copies:
+        copy.start()
+    for copy in copies:
+        copy.wait()
+    out_ref[:PATCHES, :] = rows_ref[0, :, 0, :]
+    out_ref[PART:PART + PATCHES, :] = rows_ref[1, :, 0, :]
+    out_ref[2 * PART - 8:, :] = jnp.broadcast_to(row_ref[...].astype(jnp.float32), (8, 512))
 
 
 def pack(k, v, label):
+    values = [pltpu.with_memory_space_constraint(value, pltpu.HBM) for value in (k, v, label)]
     return pl.pallas_call(
         pack_kernel,
+        in_specs=[pl.BlockSpec(memory_space=pltpu.HBM)] * 3,
+        out_specs=pl.BlockSpec(memory_space=pltpu.VMEM),
         out_shape=pltpu.VMEM((2 * PART, 512), jnp.float32),
+        scratch_shapes=[
+            pltpu.VMEM((2, PATCHES, 1, 512), jnp.float32),
+            pltpu.VMEM((1, 512), jnp.int32),
+            pltpu.SemaphoreType.DMA((3,)),
+        ],
         name="pack",
         compiler_params=PARAMS,
-    )(k, v, label)
+    )(*values)
 
 
 def prepare_image(packed_ref, kc_ref, vc_ref, kt_ref, vt_ref, pad_ref):

time: 94 us -> 93.9 us (level)
  local copies, waits for them, and re-layouts: 4.87 us -> 2.19 us
  waiting for transfers between devices: 20.7 us -> 22.2 us
  Pallas kernels: 8.58 us -> 9.72 us
    unnamed x9 -> x3, local copies, waits for them, and re-layouts: 2.68 us -> 0.01 us
    all_to_all x2, waiting for transfers between devices: 20.7 us -> 22.2 us  [spread(): lax.all_to_all(jnp.broadcast_to(value[None], (count,) + value.shape), axi...]
    pallas_call x1, Pallas kernels: 0.1 us -> 1.24 us  [pack(): pl.pallas_call(pack_kernel, in_specs=[pl.BlockSpec(memory_space=pltpu.HBM...]
  transfers between devices with their start and end apart: 4 -> 4, of which waited for: 2 -> 2; matrix products, arithmetic and copies ran while one was open for 2% -> 2% of each run, Pallas kernels for 0% -> 1%
where the time goes in v5:
time: 93.9 us; the launch traced here: 93.4 us
  blocking collectives  31.5 us (34%)
  starting transfers between devices  26.4 us (28%)
  waiting for transfers between devices  22.2 us (24%)
  Pallas kernels  9.72 us (10%)
  local copies, waits for them, and re-layouts  2.19 us (2%)
    all_to_all x2, starting transfers between devices, spread(): lax.all_to_all(jnp.broadcast_to(value[None], (count,) + value.shape), axi...  22.6 us
    all_to_all x2, waiting for transfers between devices, spread(): lax.all_to_all(jnp.broadcast_to(value[None], (count,) + value.shape), axi...  22.2 us
    all_to_all x1, blocking collectives, per_device(): lax.all_to_all(dq.reshape(16, 16, 512), RING, 0, 0, tiled=True).sum(0)  16.3 us
    all_to_all x1, blocking collectives, per_device(): lax.all_to_all(total.reshape(16, 1, 512), 'z', 0, 0, tiled=True).sum(0)  15.1 us
    pallas_call x1, Pallas kernels, grads(): pl.pallas_call(grads_kernel, in_specs=[pl.BlockSpec(memory_space=pltpu.SM...  7.5 us
    ppermute x2, starting transfers between devices, swapped(): return lax.ppermute(value, 'core', [(0, 1), (1, 0)])  3.83 us
    broadcast_in_dim x2, local copies, waits for them, and re-layouts, spread(): jnp.broadcast_to(value[None], (count,) + value.shape)  2.16 us
  transfers between devices with their start and end apart: 4, of which 2 were waited for; matrix products, arithmetic and copies ran while one was open for 2% of the time, Pallas kernels for 1%

profile of v5, /device:TPU:8, one launch (start us, length us, event | category | flops | bytes accessed | tf_op | source)
XLA Modules:
  0.0 93.4 jit_solution(14704968802445835925)
XLA Ops:
  0.6 1.3 %broadcast_in_dim.7 = f32[16,1,512]{2,1,0:T(1,128)} broadcast(f32[512]{0:T(512)} %bitcast.17), dimensions={2} | broadcast | bytes 34816 | tf_op jit(solution)/shard_map/broadcast_in_dim | solution.py:245
  1.9 15.2 %all-to-all-start = ((f32[16,1,512]{2,1,0:T(1,128)}), f32[16,1,512]{2,1,0:T(1,128)S(1)}, u32[]{:S(2)}, u32[]{:S(2)}) async-start(f32[16,1,512]{2,1,0:T(1,128)} %broadcast_in_dim.7), calls=%async_computation | async-start | bytes 65536 | tf_op jit(solution)/shard_map/all_to_all | solution.py:245
  17.1 1.2 %pack.1.refs_0_ = f32[416,512]{1,0:T(8,128)S(1)} custom-call(f32[196,1,512]{2,1,0:T(1,128)} %bitcast.14, f32[196,1,512]{2,1,0:T(1,128)} %bitcast.15, s32[1,512]{1,0:T(1,128)} %label_ref.1), custom_call_target="tpu_custom_call" | custom-call | tf_op jit(solution)/shard_map/pack/pallas_call | solution.py:49
  18.4 11.3 %all-to-all-done = f32[16,1,512]{2,1,0:T(1,128)S(1)} async-done(((f32[16,1,512]{2,1,0:T(1,128)}), f32[16,1,512]{2,1,0:T(1,128)S(1)}, u32[]{:S(2)}, u32[]{:S(2)}) %all-to-all-start) | async-done | bytes 32800 | tf_op jit(solution)/shard_map/all_to_all | solution.py:245
  29.7 1.9 %collective-permute-start = (f32[416,512]{1,0:T(8,128)S(1)}, f32[416,512]{1,0:T(8,128)S(1)}, u32[]{:S(2)}, u32[]{:S(2)}) collective-permute-start(f32[416,512]{1,0:T(8,128)S(1)} %pack.1.refs_0_), channel_id=1, source_target_pairs={{0,32},{32,0},{1,33},{33,1},{2,34},{34,2},{3,35},{35,3},{4,36},{36... | collective-permute-start | bytes 2555912 | tf_op jit(solution)/shard_map/ppermute | solution.py:249
  31.6 0.8 broadcast_in_dim.16
  32.5 7.4 %all-to-all-start.1 = ((f32[16,16,512]{2,1,0:T(8,128)}), f32[16,16,512]{2,1,0:T(8,128)S(1)}, u32[]{:S(2)}, u32[]{:S(2)}) async-start(f32[16,16,512]{2,1,0:T(8,128)} %broadcast_in_dim.16), calls=%async_computation.1 | async-start | bytes 1048576 | tf_op jit(solution)/shard_map/all_to_all | solution.py:245
  39.9 10.9 %all-to-all-done.1 = f32[16,16,512]{2,1,0:T(8,128)S(1)} async-done(((f32[16,16,512]{2,1,0:T(8,128)}), f32[16,16,512]{2,1,0:T(8,128)S(1)}, u32[]{:S(2)}, u32[]{:S(2)}) %all-to-all-start.1) | async-done | bytes 524320 | tf_op jit(solution)/shard_map/all_to_all | solution.py:245
  50.8 0.0 collective-permute-done.refs_1_
  50.8 7.5 %grads.1 = (f32[256,512]{1,0:T(8,128)}, f32[416,512]{1,0:T(8,128)}, f32[416,512]{1,0:T(8,128)S(1)}) custom-call(s32[1]{0:T(128)} %bitcast.core_ref, f32[256,512]{1,0:T(8,128)S(1)} %bitcast.12, f32[416,512]{1,0:T(8,128)S(1)} %pack.1.refs_0_, f32[416,512]{1,0:T(8,128)S(1)} %collective-permute-done.refs_1_), custom_call_target="tpu_custom_call" | custom-call | tf_op jit(solution)/shard_map/grads/pallas_call | solution.py:209
  58.3 1.9 %collective-permute-start.1 = (f32[416,512]{1,0:T(8,128)S(1)}, f32[416,512]{1,0:T(8,128)S(1)}, u32[]{:S(2)}, u32[]{:S(2)}) collective-permute-start(f32[416,512]{1,0:T(8,128)S(1)} %get-tuple-element.19), channel_id=1, source_target_pairs={{0,32},{32,0},{1,33},{33,1},{2,34},{34,2},{3,35},{35,3},{4,36},{36... | collective-permute-start | bytes 2555912 | tf_op jit(solution)/shard_map/ppermute | solution.py:249
  60.2 0.0 copy-start
  60.2 16.3 %all_to_all.20 = f32[16,16,512]{2,1,0:T(8,128)S(1)} all-to-all(f32[16,16,512]{2,1,0:T(8,128)} %bitcast.13), channel_id=1, replica_groups=mesh['y_hi'=2,'x'=4,'core'=2,'y_lo'=2,'z'=16] {'y_hi','x','y_lo'}, dimensions={0} | all-to-all | bytes 1048576 | tf_op jit(solution)/shard_map/all_to_all | solution.py:261
  76.6 15.1 %all_to_all.21 = f32[16,1,512]{2,1,0:T(1,128)S(1)} all-to-all(f32[16,1,512]{2,1,0:T(1,128)S(1)} %reshape.30), channel_id=1, replica_groups=mesh['y_hi'=2,'x'=4,'core'=2,'y_lo'=2,'z'=16] {'z'}, dimensions={0} | all-to-all | bytes 65536 | tf_op jit(solution)/shard_map/all_to_all | solution.py:263
  91.8 0.6 reduce_sum.21
  92.4 0.0 collective-permute-done.1.received_ref
  92.4 0.0 copy-done
  92.4 1.0 %finish.1 = (f32[196,1,512]{2,1,0:T(1,128)}, f32[196,1,512]{2,1,0:T(1,128)}) custom-call(f32[416,512]{1,0:T(8,128)S(1)} %copy-done, f32[416,512]{1,0:T(8,128)S(1)} %collective-permute-done.1.received_ref), custom_call_target="tpu_custom_call" | custom-call | tf_op jit(solution)/shard_map/finish/pallas_call | solution.py:236
  (3 shorter events, 0.1 us)
Async XLA Ops:
  1.9 27.8 %all-to-all-start = ((f32[16,1,512]{2,1,0:T(1,128)}), f32[16,1,512]{2,1,0:T(1,128)S(1)}, u32[]{:S(2)}, u32[]{:S(2)}) async-start(f32[16,1,512]{2,1,0:T(1,128)} %broadcast_in_dim.7), calls=%async_computation | async-start | bytes 65536 | tf_op jit(solution)/shard_map/all_to_all | solution.py:245
  29.7 21.1 %collective-permute-start = (f32[416,512]{1,0:T(8,128)S(1)}, f32[416,512]{1,0:T(8,128)S(1)}, u32[]{:S(2)}, u32[]{:S(2)}) collective-permute-start(f32[416,512]{1,0:T(8,128)S(1)} %pack.1.refs_0_), channel_id=1, source_target_pairs={{0,32},{32,0},{1,33},{33,1},{2,34},{34,2},{3,35},{35,3},{4,36},{36... | collective-permute-start | bytes 2555912 | tf_op jit(solution)/shard_map/ppermute | solution.py:249
  32.5 18.3 %all-to-all-start.1 = ((f32[16,16,512]{2,1,0:T(8,128)}), f32[16,16,512]{2,1,0:T(8,128)S(1)}, u32[]{:S(2)}, u32[]{:S(2)}) async-start(f32[16,16,512]{2,1,0:T(8,128)} %broadcast_in_dim.16), calls=%async_computation.1 | async-start | bytes 1048576 | tf_op jit(solution)/shard_map/all_to_all | solution.py:245
  58.3 34.1 %collective-permute-start.1 = (f32[416,512]{1,0:T(8,128)S(1)}, f32[416,512]{1,0:T(8,128)S(1)}, u32[]{:S(2)}, u32[]{:S(2)}) collective-permute-start(f32[416,512]{1,0:T(8,128)S(1)} %get-tuple-element.19), channel_id=1, source_target_pairs={{0,32},{32,0},{1,33},{33,1},{2,34},{34,2},{3,35},{35,3},{4,36},{36... | collective-permute-start | bytes 2555912 | tf_op jit(solution)/shard_map/ppermute | solution.py:249
  60.2 32.2 %copy-start = (f32[416,512]{1,0:T(8,128)S(1)}, f32[416,512]{1,0:T(8,128)}, u32[]{:S(2)}) copy-start(f32[416,512]{1,0:T(8,128)} %get-tuple-element.18.own_ref) | copy-start | bytes 2555908
